TPU v7x, 32 devices: a whole 2x2x4 slice. The times are simulated.
32 devices in a mesh: seq: 32 (over z, y, x, core).
Axes of the slice: x: 2, y: 2, z: 4, core: 2. Of those that a mesh axis runs over, the one named last changes fastest.
Arguments:
- tokens: bfloat16 [12288, 768], P('seq'), may hold values from -6 to 6
- cotangent: bfloat16 [12288, 768], P('seq'), may hold values from -6 to 6
- offsets: int32 [9], replicated, may hold values from 0 to 12287, as said below
- gain_in: bfloat16 [2, 768], P(None, 'seq'), may hold values from 0.099609375 to 1.8984375
- w_in: bfloat16 [2, 768, 3376], P(None, 'seq'), may hold values from -0.21875 to 0.21875
- conv_w: bfloat16 [2, 1792, 7], P(None, 'seq'), may hold values from -2 to 2
- conv_b: bfloat16 [2, 1792], P(None, 'seq'), may hold values from -3 to 3
- gain_out: bfloat16 [2, 1536], P(None, 'seq'), may hold values from 0.099609375 to 1.8984375
- w_out: bfloat16 [2, 1536, 768], P(None, 'seq'), may hold values from -0.15625 to 0.15625
- head_params: float32 [2, 4, 24], replicated, may hold values from -13 to 1.5
Outputs:
- result: bfloat16 [12288, 768], P('seq')
- grad_tokens: float32 [12288, 768], P('seq')
- grad_gain_in: float32 [2, 768], P(None, 'seq')
- grad_w_in: float32 [2, 768, 3376], P(None, 'seq')
- grad_conv_w: float32 [2, 1792, 7], P(None, 'seq')
- grad_conv_b: float32 [2, 1792], P(None, 'seq')
- grad_gain_out: float32 [2, 1536], P(None, 'seq')
- grad_w_out: float32 [2, 1536, 768], P(None, 'seq')
- grad_head_params: float32 [2, 4, 24], replicated
Inputs may be any that keep to these rules, and one draw needn't show every extreme that they name: offsets[0] = 0 and they rise strictly; offsets[8] = 12287, so the last token is padding; one sequence starts within the first 192 tokens and ends after token 12096.
All inputs are finite; a program needn't handle non-finite values.
Results may differ from a plain program's by a relative error of at most 0.025.
Values may be sent and summed in bfloat16 or wider, within the bound.
No kernel may reach another device: no remote copies, remote signals or barrier semaphores. Data moves between devices by JAX's collectives and lax.ppermute only.
A program may use at most 832 MiB of HBM per device.

v0:
```python
import jax
import jax.numpy as jnp
from jax import lax
from jax.sharding import PartitionSpec as P

HEADS = 24
HEAD = 64
STATE = 64
CONV = 4
SPAN = 128
LAYERS = 2
NSEQ = 8
INNER = 1536
CONVW = 1792


precise = lax.Precision.HIGHEST
epsilon = 1e-05


def padded(block, sides, width):
    for axis, dim in sides:
        count = lax.axis_size(axis)
        forward = [(i, i + 1) for i in range(count - 1)]
        backward = [(target, source) for source, target in forward]
        low = lax.ppermute(
            lax.slice_in_dim(block, block.shape[dim] - width, None, axis=dim), axis, forward
        )
        high = lax.ppermute(lax.slice_in_dim(block, 0, width, axis=dim), axis, backward)
        block = jnp.concatenate([low, block, high], axis=dim)
    return block


def prefix(shard, axis, combine, identity, reverse):
    count, mine = (lax.axis_size(axis), lax.axis_index(axis))
    everything = jax.tree.map(
        lambda part, kind: lax.all_gather(part.astype(kind), axis),
        shard,
        (jnp.bfloat16, jnp.bfloat16),
    )
    start = jax.tree.map(
        lambda part, zero: jnp.broadcast_to(jnp.asarray(zero, part.dtype), part.shape),
        shard,
        identity,
    )

    def hop(k, before):
        at = count - 1 - k if reverse else k
        reached = at > mine if reverse else at < mine
        new = combine(
            before, jax.tree.map(lambda part, own: part[at].astype(own.dtype), everything, shard)
        )
        return jax.tree.map(lambda a, b: jnp.where(reached, a, b), new, before)

    return lax.fori_loop(0, count, hop, start)


def carried_in(shard, axis, join, neutral, backward):
    count = lax.axis_size(axis)
    place = lax.axis_index(axis)
    ahead = count - 1 - place if backward else place
    gathered = jax.tree.map(
        lambda a, kind: lax.all_gather(a.astype(kind), axis),
        shard,
        jax.tree.map(lambda a: jnp.bfloat16 if a.dtype == jnp.float32 else a.dtype, shard),
    )
    state = jax.tree.map(lambda a, e: jnp.zeros_like(a) + jnp.asarray(e, a.dtype), shard, neutral)

    def one(hop, state):
        source = count - 1 - hop if backward else hop
        return join(
            state,
            jax.tree.map(
                lambda a, own: lax.dynamic_index_in_dim(a, source, 0, False).astype(own.dtype),
                gathered,
                shard,
            ),
        )

    return lax.fori_loop(0, ahead, one, state)


def segment_of(offsets, positions, extent):
    counted = jnp.sum((offsets[None, :] <= positions[:, None]).astype(jnp.int32), axis=1) - 1
    inside = jnp.where(positions < 0, -1, counted)
    return jnp.where(positions >= extent, -2, inside)


def rounded(tensor):
    return lax.optimization_barrier(tensor.astype(jnp.bfloat16)).astype(jnp.float32)


def norm_scale(hidden):
    return lax.rsqrt(jnp.mean(hidden * hidden, axis=1, keepdims=True) + epsilon)


def combine_states(earlier, later):
    return (earlier[0] * later[0], later[0][:, None, None] * earlier[1] + later[1])


def block_step(carried, block_data):
    state_now, previous = carried
    values, writes, reads, steps, decays, labels = block_data
    extent = labels.shape[0]
    cumulative = jnp.cumsum(decays, axis=0)
    scores = jnp.dot(reads, writes.T, precision=precise)
    places = jnp.arange(extent)
    linked = (labels[:, None] == labels[None, :]) & (places[:, None] > places[None, :])
    cum_heads = cumulative.T
    log_gap = jnp.minimum(cum_heads[:, :, None] - cum_heads[:, None, :], 0.0)
    mixing = jnp.where(linked[None, :, :], jnp.exp(log_gap), 0.0) * scores[None, :, :]
    inputs = values * steps[:, :, None]
    within = jnp.einsum("hts,shp->thp", mixing, inputs, precision=precise)
    entering = jnp.where((labels == previous)[:, None], jnp.exp(cumulative), 0.0)
    from_state = (
        jnp.einsum("tn,hpn->thp", reads, state_now, precision=precise) * entering[:, :, None]
    )
    final_label = labels[extent - 1]
    trailing = jnp.where(
        (labels == final_label)[:, None], jnp.exp(cumulative[extent - 1][None, :] - cumulative), 0.0
    )
    through = jnp.where(final_label == previous, jnp.exp(cumulative[extent - 1]), 0.0)
    added_state = jnp.einsum("sh,shp,sn->hpn", trailing, inputs, writes, precision=precise)
    return ((state_now * through[:, None, None] + added_state, final_label), within + from_state)


def scan_direction(step_function, values, writes, reads, steps, decays, labels, previous, state_in):
    number = labels.shape[0] // SPAN

    def blocked(tensor):
        return tensor.reshape((number, SPAN) + tensor.shape[1:])

    final_carry, outputs = lax.scan(
        step_function,
        (state_in, previous),
        (
            blocked(values),
            blocked(writes),
            blocked(reads),
            blocked(steps),
            blocked(decays),
            blocked(labels),
        ),
    )
    return (outputs.reshape(values.shape), final_carry[0])


def conv_mix(bordered, conv_w, conv_b, labels, labels_rim):
    extent = labels.shape[0]
    pre_act = jnp.zeros((extent, conv_b.shape[0]), jnp.float32) + conv_b[None, :]
    for tap_index in range(2 * CONV - 1):
        linked = (labels_rim[tap_index : tap_index + extent] == labels).astype(jnp.float32)
        pre_act = (
            pre_act
            + conv_w[:, tap_index][None, :]
            * bordered[tap_index : tap_index + extent]
            * linked[:, None]
        )
    return pre_act


def entering_weights(decays, labels, outer_label):
    return jnp.where((labels == outer_label)[:, None], jnp.exp(jnp.cumsum(decays, axis=0)), 0.0)


def inject(reads, decays, labels, outer_label, state_in):
    return (
        jnp.einsum("tn,hpn->thp", reads, state_in, precision=precise)
        * entering_weights(decays, labels, outer_label)[:, :, None]
    )


def whole_decay(decays, labels, outer_label):
    extent = labels.shape[0]
    return jnp.where(labels[extent - 1] == outer_label, jnp.exp(jnp.sum(decays, axis=0)), 0.0)


def mixer_inputs(projected, bordered, conv_w, conv_b, head_table, context):
    labels, labels_rim, present, left_label, right_label = context
    extent = projected.shape[0]
    pre_act = conv_mix(
        bordered.astype(jnp.float32),
        conv_w.astype(jnp.float32),
        conv_b.astype(jnp.float32),
        labels,
        labels_rim,
    )
    activated = rounded(jax.nn.silu(pre_act) * present[:, None])
    values = activated[:, :INNER].reshape(extent, HEADS, HEAD)
    decay_rate = jnp.exp(head_table[0])
    raw_steps = projected[:, INNER + CONVW :]
    step_fore = jax.nn.softplus(raw_steps[:, :HEADS] + head_table[1][None, :])
    step_back = jax.nn.softplus(raw_steps[:, HEADS:] + head_table[2][None, :])
    forward_args = (
        values,
        activated[:, INNER : INNER + STATE],
        activated[:, INNER + STATE : INNER + 2 * STATE],
        step_fore,
        -decay_rate[None, :] * step_fore,
    )
    reverse_args = (
        values[::-1],
        activated[::-1, INNER + 2 * STATE : INNER + 3 * STATE],
        activated[::-1, INNER + 3 * STATE :],
        step_back[::-1],
        (-decay_rate[None, :] * step_back)[::-1],
    )
    return (pre_act, values, forward_args, reverse_args)


def layer_forward(hidden, weights, head_table, context):
    gain_in, w_in, conv_w, conv_b, gain_out, w_out = weights
    labels, labels_rim, present, left_label, right_label = context
    extent = hidden.shape[0]
    normed_in = (hidden * norm_scale(hidden) * gain_in.astype(jnp.float32)[None, :]).astype(
        jnp.bfloat16
    )
    projected = jnp.dot(normed_in, w_in, preferred_element_type=jnp.float32)
    channels = projected[:, INNER : INNER + CONVW].astype(jnp.bfloat16)
    bordered = padded(channels, (("seq", 0),), CONV - 1)
    pre_act, values, forward_args, reverse_args = mixer_inputs(
        projected, bordered, conv_w, conv_b, head_table, context
    )
    zero_state = jnp.zeros((HEADS, HEAD, STATE), jnp.float32)
    identity = (jnp.ones((HEADS,), jnp.float32), zero_state)
    start_fore, state_fore = scan_direction(
        block_step, *forward_args, labels, left_label, zero_state
    )
    total_fore = whole_decay(forward_args[4], labels, left_label)
    entry_fore = prefix((total_fore, state_fore), "seq", combine_states, identity, False)[1]
    mixed_fore = start_fore + inject(
        forward_args[2], forward_args[4], labels, left_label, entry_fore
    )
    labels_back = labels[::-1]
    start_back, state_back = scan_direction(
        block_step, *reverse_args, labels_back, right_label, zero_state
    )
    total_back = whole_decay(reverse_args[4], labels_back, right_label)
    entry_back = prefix((total_back, state_back), "seq", combine_states, identity, True)[1]
    mixed_back = start_back + inject(
        reverse_args[2], reverse_args[4], labels_back, right_label, entry_back
    )
    merged = mixed_fore + mixed_back[::-1] + head_table[3][None, :, None] * values
    gate_values = projected[:, :INNER].reshape(extent, HEADS, HEAD)
    gated_heads = merged * jax.nn.silu(gate_values)
    head_scale = lax.rsqrt(jnp.mean(gated_heads * gated_heads, axis=2, keepdims=True) + epsilon)
    normed_out = (
        (gated_heads * head_scale).reshape(extent, INNER) * gain_out.astype(jnp.float32)[None, :]
    ).astype(jnp.bfloat16)
    branch = jnp.dot(normed_out, w_out, preferred_element_type=jnp.float32)
    return (hidden + branch, (hidden, normed_in, projected, bordered, entry_fore, entry_back))


def layer_backward(grad_out, stored, weights, head_table, context):
    hidden, normed_in, projected, bordered, entry_fore, entry_back = stored
    gain_in, w_in, conv_w, conv_b, gain_out, w_out = weights
    labels, labels_rim, present, left_label, right_label = context
    extent = hidden.shape[0]
    gain_in_f = gain_in.astype(jnp.float32)
    gain_out_f = gain_out.astype(jnp.float32)
    pre_act, values, forward_args, reverse_args = mixer_inputs(
        projected, bordered, conv_w, conv_b, head_table, context
    )
    labels_back = labels[::-1]
    zero_state = jnp.zeros((HEADS, HEAD, STATE), jnp.float32)
    identity = (jnp.ones((HEADS,), jnp.float32), zero_state)

    def run_fore(values_in, writes, reads, steps, decays):
        return scan_direction(
            block_step, values_in, writes, reads, steps, decays, labels, left_label, entry_fore
        )

    def run_back(values_in, writes, reads, steps, decays):
        return scan_direction(
            block_step,
            values_in,
            writes,
            reads,
            steps,
            decays,
            labels_back,
            right_label,
            entry_back,
        )

    outputs_fore, pull_fore = jax.vjp(run_fore, *forward_args)
    outputs_back, pull_back = jax.vjp(run_back, *reverse_args)
    merged = outputs_fore[0] + outputs_back[0][::-1] + head_table[3][None, :, None] * values
    gate_values = projected[:, :INNER].reshape(extent, HEADS, HEAD)
    gate_sigmoid = jax.nn.sigmoid(gate_values)
    gate_silu = gate_values * gate_sigmoid
    gated_heads = merged * gate_silu
    head_scale = lax.rsqrt(jnp.mean(gated_heads * gated_heads, axis=2, keepdims=True) + epsilon)
    normed_heads = (gated_heads * head_scale).reshape(extent, INNER)
    normed_out = (normed_heads * gain_out_f[None, :]).astype(jnp.bfloat16)
    grad_branch = grad_out.astype(jnp.bfloat16)
    grad_w_out = jnp.dot(normed_out.T, grad_branch, preferred_element_type=jnp.float32)
    grad_normed = jnp.dot(grad_branch, w_out.T, preferred_element_type=jnp.float32)
    grad_gain_out = jnp.sum(grad_normed * normed_heads, axis=0)
    scaled = (grad_normed * gain_out_f[None, :]).reshape(extent, HEADS, HEAD)
    grad_gated = head_scale * scaled - gated_heads * head_scale**3 * jnp.mean(
        scaled * gated_heads, axis=2, keepdims=True
    )
    grad_merged = grad_gated * gate_silu
    grad_gate = grad_gated * merged * gate_sigmoid * (1.0 + gate_values * (1.0 - gate_sigmoid))
    grad_skip = jnp.sum(grad_merged * values, axis=(0, 2))
    total_fore = whole_decay(forward_args[4], labels, left_label)
    source_fore = jnp.einsum(
        "th,thp,tn->hpn",
        entering_weights(forward_args[4], labels, left_label),
        grad_merged,
        forward_args[2],
        precision=precise,
    )
    adjoint_fore = carried_in((total_fore, source_fore), "seq", combine_states, identity, True)[1]
    grads_fore = pull_fore((grad_merged, adjoint_fore))
    grad_merged_back = grad_merged[::-1]
    total_back = whole_decay(reverse_args[4], labels_back, right_label)
    source_back = jnp.einsum(
        "th,thp,tn->hpn",
        entering_weights(reverse_args[4], labels_back, right_label),
        grad_merged_back,
        reverse_args[2],
        precision=precise,
    )
    adjoint_back = carried_in((total_back, source_back), "seq", combine_states, identity, False)[1]
    grads_back = pull_back((grad_merged_back, adjoint_back))
    decay_rate = jnp.exp(head_table[0])
    grad_values = grads_fore[0] + grads_back[0][::-1] + head_table[3][None, :, None] * grad_merged
    grad_step_fore = grads_fore[3] - decay_rate[None, :] * grads_fore[4]
    grad_step_back = (grads_back[3] - decay_rate[None, :] * grads_back[4])[::-1]
    grad_rate_log = jnp.sum(grads_fore[4] * forward_args[4], axis=0) + jnp.sum(
        grads_back[4] * reverse_args[4], axis=0
    )
    raw_steps = projected[:, INNER + CONVW :]
    grad_raw_fore = grad_step_fore * jax.nn.sigmoid(raw_steps[:, :HEADS] + head_table[1][None, :])
    grad_raw_back = grad_step_back * jax.nn.sigmoid(raw_steps[:, HEADS:] + head_table[2][None, :])
    grad_act = jnp.concatenate(
        [
            grad_values.reshape(extent, INNER),
            grads_fore[1],
            grads_fore[2],
            grads_back[1][::-1],
            grads_back[2][::-1],
        ],
        axis=1,
    )
    pre_sigmoid = jax.nn.sigmoid(pre_act)
    grad_pre = (
        grad_act * present[:, None] * pre_sigmoid * (1.0 + pre_act * (1.0 - pre_sigmoid))
    ).astype(jnp.bfloat16)
    bordered_grad = padded(grad_pre, (("seq", 0),), CONV - 1).astype(jnp.float32)
    border_rows = bordered.astype(jnp.float32)
    pre_grad_wide = grad_pre.astype(jnp.float32)
    tap_weights = conv_w.astype(jnp.float32)
    grad_channels = jnp.zeros((extent, CONVW), jnp.float32)
    tap_grads = []
    for tap_index in range(2 * CONV - 1):
        linked = (labels_rim[tap_index : tap_index + extent] == labels).astype(jnp.float32)
        tap_grads.append(
            jnp.sum(
                pre_grad_wide * border_rows[tap_index : tap_index + extent] * linked[:, None],
                axis=0,
            )
        )
        mirror = 2 * (CONV - 1) - tap_index
        linked_back = (labels_rim[mirror : mirror + extent] == labels).astype(jnp.float32)
        grad_channels = (
            grad_channels
            + tap_weights[:, tap_index][None, :]
            * bordered_grad[mirror : mirror + extent]
            * linked_back[:, None]
        )
    grad_conv_w = jnp.stack(tap_grads, axis=1)
    grad_conv_b = jnp.sum(pre_grad_wide, axis=0)
    grad_proj = jnp.concatenate(
        [grad_gate.reshape(extent, INNER), grad_channels, grad_raw_fore, grad_raw_back], axis=1
    ).astype(jnp.bfloat16)
    grad_w_in = jnp.dot(normed_in.T, grad_proj, preferred_element_type=jnp.float32)
    grad_normed_in = jnp.dot(grad_proj, w_in.T, preferred_element_type=jnp.float32)
    factor = norm_scale(hidden)
    grad_gain_in = jnp.sum(grad_normed_in * hidden * factor, axis=0)
    scaled_in = grad_normed_in * gain_in_f[None, :]
    grad_hidden = (
        grad_out
        + factor * scaled_in
        - hidden * factor**3 * jnp.mean(scaled_in * hidden, axis=1, keepdims=True)
    )
    head_grad = jnp.stack(
        [grad_rate_log, jnp.sum(grad_raw_fore, axis=0), jnp.sum(grad_raw_back, axis=0), grad_skip]
    )
    return (
        grad_hidden,
        (grad_gain_in, grad_w_in, grad_conv_w, grad_conv_b, grad_gain_out, grad_w_out),
        head_grad,
    )


def shards(tokens, cotangent, offsets, gain_in, w_in, conv_w, conv_b, gain_out, w_out, head_params):
    length = tokens.shape[0]
    anchor = lax.axis_index("seq") * length
    grid_size = lax.axis_size("seq") * length
    positions = anchor + jnp.arange(length, dtype=jnp.int32)
    labels = segment_of(offsets, positions, grid_size)
    labels_rim = segment_of(
        offsets, anchor + jnp.arange(-(CONV - 1), length + CONV - 1, dtype=jnp.int32), grid_size
    )
    present = (positions < offsets[NSEQ]).astype(jnp.float32)
    left_label = labels_rim[CONV - 2]
    right_label = labels_rim[length + CONV - 1]
    context = (labels, labels_rim, present, left_label, right_label)
    hidden = tokens.astype(jnp.float32)
    storage = []
    fetched = []
    for layer_index in range(LAYERS):
        weights = (
            lax.all_gather(gain_in[layer_index], "seq", axis=0, tiled=True),
            lax.all_gather(w_in[layer_index], "seq", axis=0, tiled=True),
            lax.all_gather(conv_w[layer_index], "seq", axis=0, tiled=True),
            lax.all_gather(conv_b[layer_index], "seq", axis=0, tiled=True),
            lax.all_gather(gain_out[layer_index], "seq", axis=0, tiled=True),
            lax.all_gather(w_out[layer_index], "seq", axis=0, tiled=True),
        )
        hidden, stored = layer_forward(hidden, weights, head_params[layer_index], context)
        storage.append(stored)
        fetched.append(weights)
    result = hidden.astype(jnp.bfloat16)
    gradient = cotangent.astype(jnp.float32)
    shares = [None] * LAYERS
    head_terms = [None] * LAYERS
    for layer_index in reversed(range(LAYERS)):
        weights = (
            lax.all_gather(gain_in[layer_index], "seq", axis=0, tiled=True),
            lax.all_gather(w_in[layer_index], "seq", axis=0, tiled=True),
            lax.all_gather(conv_w[layer_index], "seq", axis=0, tiled=True),
            lax.all_gather(conv_b[layer_index], "seq", axis=0, tiled=True),
            lax.all_gather(gain_out[layer_index], "seq", axis=0, tiled=True),
            lax.all_gather(w_out[layer_index], "seq", axis=0, tiled=True),
        )
        gradient, local_grads, head_terms[layer_index] = layer_backward(
            gradient, storage[layer_index], weights, head_params[layer_index], context
        )
        grad_gain_in, grad_w_in, grad_conv_w, grad_conv_b, grad_gain_out, grad_w_out = local_grads
        shares[layer_index] = (
            lax.psum_scatter(grad_gain_in, "seq", scatter_dimension=0, tiled=True),
            lax.psum_scatter(grad_w_in, "seq", scatter_dimension=0, tiled=True),
            lax.psum_scatter(grad_conv_w, "seq", scatter_dimension=0, tiled=True),
            lax.psum_scatter(grad_conv_b, "seq", scatter_dimension=0, tiled=True),
            lax.psum_scatter(grad_gain_out, "seq", scatter_dimension=0, tiled=True),
            lax.psum_scatter(grad_w_out, "seq", scatter_dimension=0, tiled=True),
        )
    head_total = lax.psum(jnp.stack(head_terms), "seq")
    stacked = [
        jnp.stack([shares[layer_index][member] for layer_index in range(LAYERS)])
        for member in range(6)
    ]
    return (
        result,
        gradient,
        stacked[0],
        stacked[1],
        stacked[2],
        stacked[3],
        stacked[4],
        stacked[5],
        head_total,
    )


def solution(mesh):
    in_specs = (
        P("seq", None),
        P("seq", None),
        P(),
        P(None, "seq"),
        P(None, "seq", None),
        P(None, "seq", None),
        P(None, "seq"),
        P(None, "seq"),
        P(None, "seq", None),
        P(),
    )
    out_specs = (
        P("seq", None),
        P("seq", None),
        P(None, "seq"),
        P(None, "seq", None),
        P(None, "seq", None),
        P(None, "seq"),
        P(None, "seq"),
        P(None, "seq", None),
        P(),
    )
    return jax.shard_map(shards, mesh=mesh, in_specs=in_specs, out_specs=out_specs, check_vma=False)
```

profile of v0, /device:TPU:0, one launch (start us, length us, event | category | flops | bytes accessed | tf_op | source)
XLA Modules:
  0.0 3639.2 jit_solution(2820872718914295920)
XLA Ops:
  10.1 42.9 %all-reduce.8 = bf16[768]{0:T(1024)(128)(2,1)S(1)} all-reduce(bf16[768]{0:T(1024)(128)(2,1)S(1)} %dynamic-update-slice), channel_id=2, replica_groups=mesh['seq'=32] {'seq'}, use_global_device_ids=true, to_apply=%add.8 | all-reduce | flops 768 | bytes 3072
  61.6 43.1 %all-gather.3 = bf16[1,1792,7]{2,0,1:T(2,128)(2,1)S(1)} all-gather(bf16[1,56,7]{2,0,1:T(2,128)(2,1)S(1)} %copy.1109), channel_id=5, replica_groups=mesh['seq'=32] {'seq'}, dimensions={1}, use_global_device_ids=true | all-gather | bytes 25872 | tf_op jit(solution)/shard_map/all_gather | solution.py:419
  130.4 38.4 %all-reduce.30 = (bf16[1792]{0:T(1024)(128)(2,1)S(1)}, bf16[768]{0:T(1024)(128)(2,1)}, bf16[768]{0:T(1024)(128)(2,1)}, bf16[1536]{0:T(1024)(128)(2,1)}, bf16[768]{0:T(1024)(128)(2,1)}) all-reduce(bf16[1792]{0:T(1024)(128)(2,1)S(1)} %dynamic-update-slice.1, bf16[768]{0:T(1024)(128)(2,1)S(1)} %dynamic-update-slice.3, ...), channel_id=4, replica_groups=mesh['seq'=32] {'seq'}, use_global_device_ids=true, to_apply=%add.9 | all-reduce | flops 5632 | bytes 22528
  190.2 108.4 %while.516 = (s32[]{:T(128)}, f32[24,64,64]{2,1,0:T(8,128)S(1)}, s32[]{:T(128)}, f32[3,128,24,64]{1,0,3,2:T(4,128)}, s32[3,128]{1,0:T(4,128)}, /*index=5*/f32[3,...) while((s32[]{:T(128)}, f32[24,64,64]{2,1,0:T(8,128)S(1)}, ...), condition=%wide.region_5.6_spmd.clone, body=%wide.region_3.5_spmd.clone.sunk | while | flops 619960576 | bytes 8029862 | solution.py:133
  319.7 121.2 %while.518 = (s32[]{:T(128)}, f32[24,64,64]{2,1,0:T(8,128)S(1)}, s32[]{:T(128)}, f32[3,128,24,64]{1,0,3,2:T(4,128)}, s32[3,128]{1,0:T(4,128)}, /*index=5*/f32[3,...) while((s32[]{:T(128)}, f32[24,64,64]{2,1,0:T(8,128)S(1)}, ...), condition=%wide.region_13.14_spmd.clone, body=%wide.region_11.13_spmd.clone.sunk | while | flops 619960576 | bytes 7691026 | solution.py:133
  376.3 20.2 dynamic_update_slice.1070
  449.6 47.8 %all-gather.13 = bf16[1,1792,7]{2,0,1:T(2,128)(2,1)S(1)} all-gather(bf16[1,56,7]{2,0,1:T(2,128)(2,1)S(1)} %copy.1110), channel_id=15, replica_groups=mesh['seq'=32] {'seq'}, dimensions={1}, use_global_device_ids=true | all-gather | bytes 25872 | tf_op jit(solution)/shard_map/all_gather | solution.py:419
  515.3 39.3 %while.517 = (s32[]{:T(128)}, f32[24,64,64]{2,1,0:T(8,128)S(1)}, s32[]{:T(128)}, bf16[32,24]{1,0:T(8,128)(2,1)S(1)}, bf16[32,24,64,64]{3,2,1,0:T(8,128)(2,1)}, /*index=5*/s32[]{:T(128)}, s32[]{:T(128)}) while((s32[]{:T(128)}, f32[24,64,64]{2,1,0:T(8,128)S(1)}, s32[]{:T(128)}, bf16[32,24]{1,0:T(8,128)(2,1)S(1)}, ...), condition=%wide.region_8.9_spmd.clone, body=%wide.region_7.8_spmd.clone.sunk | while | flops 491548 | bytes 983385 | solution.py:55
  555.1 39.6 %while.519 = (s32[]{:T(128)}, f32[24,64,64]{2,1,0:T(8,128)S(1)}, s32[]{:T(128)}, bf16[32,24]{1,0:T(8,128)(2,1)S(1)}, bf16[32,24,64,64]{3,2,1,0:T(8,128)(2,1)}, /*index=5*/s32[]{:T(128)}, s32[]{:T(128)}, s32[]{:T(128)}, s32[]{:T(128)}) while((s32[]{:T(128)}, f32[24,64,64]{2,1,0:T(8,128)S(1)}, s32[]{:T(128)}, ...), condition=%wide.region_16.17_spmd.clone, body=%wide.region_15.16_spmd.clone.sunk | while | flops 491552 | bytes 983447 | solution.py:55
  617.7 53.5 %all-gather.45.cloned.1.call-done = bf16[1,768,3376]{2,1,0:T(8,128)(2,1)} async-done(((bf16[1,24,3376]{2,1,0:T(8,128)(2,1)}), bf16[1,768,3376]{2,1,0:T(8,128)(2,1)}) %all-gather.45.cloned.1.call-update) | async-done | bytes 5185552 | tf_op jit(solution)/shard_map/all_gather | solution.py:418
  690.7 43.8 %all-reduce.29 = (bf16[1792]{0:T(1024)(128)(2,1)S(1)}, bf16[768]{0:T(1024)(128)(2,1)}, bf16[768]{0:T(1024)(128)(2,1)}, bf16[1536]{0:T(1024)(128)(2,1)}) all-reduce(bf16[1792]{0:T(1024)(128)(2,1)S(1)} %dynamic-update-slice.6, bf16[768]{0:T(1024)(128)(2,1)S(1)} %dynamic-update-slice.8, ...), channel_id=14, replica_groups=mesh['seq'=32] {'seq'}, use_global_device_ids=true, to_apply=%add.14 | all-reduce | flops 4864 | bytes 19456
  759.7 124.3 %while.522 = (s32[]{:T(128)}, f32[24,64,64]{2,1,0:T(8,128)}, s32[]{:T(128)}, f32[3,128,24,64]{1,0,3,2:T(4,128)}, s32[3,128]{1,0:T(4,128)}, /*index=5*/f32[3,128,...) while((s32[]{:T(128)}, f32[24,64,64]{2,1,0:T(8,128)}, ...), condition=%wide.region_31.32_spmd.clone, body=%wide.region_29.31_spmd.clone.sunk | while | flops 619960576 | bytes 8084242 | solution.py:133
  915.8 186.8 %while.514 = (s32[]{:T(128)}, f32[24,64,64]{2,1,0:T(8,128)S(1)}, s32[]{:T(128)}, f32[3,128,24,64]{1,0,3,2:T(4,128)}, f32[3,64,128]{2,1,0:T(8,128)}, /*index=5*/f...) while((s32[]{:T(128)}, f32[24,64,64]{2,1,0:T(8,128)S(1)}, ...), condition=%wide.region_73.74_spmd.clone, body=%wide.region_71.73_spmd.clone.sunk | while | flops 623508736 | bytes 19952380 | solution.py:133
  931.1 20.3 dynamic_update_slice.1051
  1129.1 119.0 %while.520 = (s32[]{:T(128)}, f32[24,64,64]{2,1,0:T(8,128)S(1)}, s32[]{:T(128)}, f32[3,128,24,64]{1,0,3,2:T(4,128)}, s32[3,128]{1,0:T(4,128)}, /*index=5*/f32[3,...) while((s32[]{:T(128)}, f32[24,64,64]{2,1,0:T(8,128)S(1)}, ...), condition=%wide.region_23.24_spmd.clone, body=%wide.region_21.23_spmd.clone.sunk | while | flops 619960576 | bytes 8083734 | solution.py:133
  1249.8 95.6 %while.523 = (s32[]{:T(128)}, f32[24,64,64]{2,1,0:T(8,128)}, s32[]{:T(128)}, bf16[32,24]{1,0:T(8,128)(2,1)}, bf16[32,24,64,64]{3,2,1,0:T(8,128)(2,1)}, /*index=5*/s32[]{:T(128)}, s32[]{:T(128)}, s32[]{:T(128)}, s32[]{:T(128)}) while((s32[]{:T(128)}, f32[24,64,64]{2,1,0:T(8,128)}, s32[]{:T(128)}, bf16[32,24]{1,0:T(8,128)(2,1)}, ...), condition=%wide.region_34.35_spmd.clone, body=%wide.region_33.34_spmd.clone.sunk | while | flops 491552 | bytes 983447 | solution.py:55
  1375.7 185.7 %while.513 = (s32[]{:T(128)}, f32[24,64,64]{2,1,0:T(8,128)S(1)}, s32[]{:T(128)}, f32[3,128,24,64]{1,0,3,2:T(4,128)}, f32[3,64,128]{2,1,0:T(8,128)}, /*index=5*/f...) while((s32[]{:T(128)}, f32[24,64,64]{2,1,0:T(8,128)S(1)}, ...), condition=%wide.region_43.44_spmd.clone, body=%wide.region_41.43_spmd.clone.sunk | while | flops 623508736 | bytes 19952380 | solution.py:133
  1572.0 59.7 %while.521 = (s32[]{:T(128)}, f32[24,64,64]{2,1,0:T(8,128)S(1)}, s32[]{:T(128)}, bf16[32,24]{1,0:T(8,128)(2,1)}, bf16[32,24,64,64]{3,2,1,0:T(8,128)(2,1)}, /*index=5*/s32[]{:T(128)}, s32[]{:T(128)}) while((s32[]{:T(128)}, f32[24,64,64]{2,1,0:T(8,128)S(1)}, s32[]{:T(128)}, bf16[32,24]{1,0:T(8,128)(2,1)}, ...), condition=%wide.region_26.27_spmd.clone, body=%wide.region_25.26_spmd.clone.sunk | while | flops 491548 | bytes 983385 | solution.py:55
  1660.9 185.9 %while.512 = (s32[]{:T(128)}, f32[24,64,64]{2,1,0:T(8,128)S(1)}, s32[]{:T(128)}, f32[3,128,24,64]{1,0,3,2:T(4,128)}, f32[3,64,128]{2,1,0:T(8,128)}, /*index=5*/f...) while((s32[]{:T(128)}, f32[24,64,64]{2,1,0:T(8,128)S(1)}, ...), condition=%wide.region_40.41_spmd.clone, body=%wide.region_38.40_spmd.clone.sunk | while | flops 623508736 | bytes 19952380 | solution.py:133
  1898.0 189.8 %while.515 = (s32[]{:T(128)}, f32[24,64,64]{2,1,0:T(8,128)S(1)}, s32[]{:T(128)}, f32[3,128,24,64]{1,0,3,2:T(4,128)}, f32[3,64,128]{2,1,0:T(8,128)}, /*index=5*/f...) while((s32[]{:T(128)}, f32[24,64,64]{2,1,0:T(8,128)S(1)}, ...), condition=%wide.region_76.77_spmd.clone, body=%wide.region_74.76_spmd.clone.sunk | while | flops 623508736 | bytes 19559164 | solution.py:133
  1914.3 20.2 dynamic_update_slice.1066
  2111.6 180.1 %while.507 = (s32[]{:T(128)}, f32[24,64,64]{2,1,0:T(8,128)S(1)}, f32[3,128,24,64]{1,0,3,2:T(4,128)}, f32[3,128,64]{1,0,2:T(4,128)}, f32[3,128,64]{1,0,2:T(4,128)...) while((s32[]{:T(128)}, f32[24,64,64]{2,1,0:T(8,128)S(1)}, ...), condition=%wide.region_69.70_spmd, body=%wide.region_60.69_spmd.sunk | while | flops 1239244800 | bytes 30558932 | solution.py:133
  2199.7 20.2 dynamic_update_slice.995
  2299.1 58.5 %while.504 = (s32[]{:T(128)}, f32[24,64,64]{2,1,0:T(8,128)S(1)}, s32[]{:T(128)}, bf16[32,24]{1,0:T(8,128)(2,1)}, bf16[32,24,64,64]{3,2,1,0:T(8,128)(2,1)}, /*index=5*/s32[]{:T(128)}, s32[]{:T(128)}, s32[]{:T(128)}, s32[]{:T(128)}) while((s32[]{:T(128)}, f32[24,64,64]{2,1,0:T(8,128)S(1)}, s32[]{:T(128)}, bf16[32,24]{1,0:T(8,128)(2,1)}, ...), condition=%wide.region_47.48_spmd, body=%wide.region_46.47_spmd.sunk | while | flops 294942 | bytes 983427 | solution.py:80
  2362.6 180.7 %while.505 = (s32[]{:T(128)}, f32[24,64,64]{2,1,0:T(8,128)S(1)}, f32[3,128,24,64]{1,0,3,2:T(4,128)}, f32[3,128,64]{1,0,2:T(4,128)}, f32[3,128,64]{1,0,2:T(4,128)...) while((s32[]{:T(128)}, f32[24,64,64]{2,1,0:T(8,128)S(1)}, ...), condition=%wide.region_57.58_spmd, body=%wide.region_48.57_spmd.sunk | while | flops 1239244800 | bytes 30411448 | solution.py:133
  2659.8 66.1 %all-gather.59.cloned.1.call-done = bf16[768,64,64]{2,1,0:T(8,128)(2,1)} async-done(((bf16[24,64,64]{2,1,0:T(8,128)(2,1)}), bf16[768,64,64]{2,1,0:T(8,128)(2,1)}) %all-gather.59.cloned.1.call-update) | async-done | bytes 6291472 | tf_op jit(solution)/shard_map/all_gather | solution.py:63
  2730.3 178.5 %while.511 = (s32[]{:T(128)}, f32[24,64,64]{2,1,0:T(8,128)S(1)}, f32[3,128,24,64]{1,0,3,2:T(4,128)}, f32[3,128,64]{1,0,2:T(4,128)}, f32[3,128,64]{1,0,2:T(4,128)...) while((s32[]{:T(128)}, f32[24,64,64]{2,1,0:T(8,128)S(1)}, ...), condition=%wide.region_102.103_spmd, body=%wide.region_93.102_spmd.sunk | while | flops 1239244800 | bytes 30218964 | solution.py:133
  2909.5 58.7 %while.508 = (s32[]{:T(128)}, f32[24,64,64]{2,1,0:T(8,128)S(1)}, s32[]{:T(128)}, bf16[32,24]{1,0:T(8,128)(2,1)}, bf16[32,24,64,64]{3,2,1,0:T(8,128)(2,1)}, /*index=5*/s32[]{:T(128)}, s32[]{:T(128)}, s32[]{:T(128)}, s32[]{:T(128)}) while((s32[]{:T(128)}, f32[24,64,64]{2,1,0:T(8,128)S(1)}, s32[]{:T(128)}, bf16[32,24]{1,0:T(8,128)(2,1)}, ...), condition=%wide.region_80.81_spmd, body=%wide.region_79.80_spmd.sunk | while | flops 294942 | bytes 983427 | solution.py:80
  2972.6 177.3 %while.509 = (s32[]{:T(128)}, f32[24,64,64]{2,1,0:T(8,128)S(1)}, f32[3,128,24,64]{1,0,3,2:T(4,128)}, f32[3,128,64]{1,0,2:T(4,128)S(1)}, f32[3,128,64]{1,0,2:T(4,...) while((s32[]{:T(128)}, f32[24,64,64]{2,1,0:T(8,128)S(1)}, ...), condition=%wide.region_90.91_spmd, body=%wide.region_81.90_spmd.sunk | while | flops 1239244800 | bytes 30018232 | solution.py:133
  3255.3 76.0 %all-reduce.33.cloned.1.call-done = (f32[768]{0:T(1024)}, f32[768]{0:T(1024)}, f32[1792,7]{0,1:T(8,128)}, f32[1792,7]{0,1:T(8,128)}, f32[1792]{0:T(1024)}, /*ind...) async-done(((f32[768]{0:T(1024)}, f32[768]{0:T(1024)}, f32[1792,7]{0,1:T(8,128)}, f32[1792,7]{0,1:T(8,128)}, f32[1792]{0:T(1024)}, ...) | async-done | bytes 133904
  3339.7 141.6 %reduce-scatter.17.cloned.1.call-done = f32[24,3376]{1,0:T(8,128)} async-done(((f32[768,3376]{1,0:T(8,128)}), f32[24,3376]{1,0:T(8,128)}) %reduce-scatter.17.cloned.1.call-update) | async-done | bytes 324112
  3481.3 147.9 %reduce-scatter.15.cloned.1.call-done = f32[24,3376]{1,0:T(8,128)} async-done(((f32[768,3376]{1,0:T(8,128)}), f32[24,3376]{1,0:T(8,128)}) %reduce-scatter.15.cloned.1.call-update) | async-done | bytes 324112
  (2583 shorter events, 2791.7 us)
Async XLA Ops:
  7.2 104.9 %all-gather.37.cloned.1.call-start = ((), (), s32[]{:S(2)}) async-start(), calls=%async_computation.6 | async-start | bytes 5474304 | tf_op jit(solution)/shard_map/all_gather | solution.py:418
  9.1 506.2 %all-gather.39.cloned.1.call-start = ((), (), s32[]{:S(2)}) async-start(), calls=%async_computation.7 | async-start | bytes 12976128 | tf_op jit(solution)/shard_map/all_gather | solution.py:37
  124.7 44.9 %collective-permute-start = (bf16[3,1792]{0,1:T(8,128)(2,1)}, bf16[3,1792]{0,1:T(8,128)(2,1)S(1)}, u32[]{:S(2)}, u32[]{:S(2)}) collective-permute-start(bf16[3,1792]{0,1:T(8,128)(2,1)} %get-tuple-element.7887), channel_id=1, source_target_pairs={{0,1},{1,2},{2,3},{3,4},{4,5},{5,6},{6,7},{7,8},{8,9},{9,10},{10,1... | collective-permute-start | bytes 32264 | tf_op jit(solution)/shard_map/ppermute | solution.py:26
  127.0 42.6 %collective-permute-start.1 = (bf16[3,1792]{0,1:T(8,128)(2,1)}, bf16[3,1792]{0,1:T(8,128)(2,1)S(1)}, u32[]{:S(2)}, u32[]{:S(2)}) collective-permute-start(bf16[3,1792]{0,1:T(8,128)(2,1)} %get-tuple-element.7888), channel_id=1, source_target_pairs={{1,0},{2,1},{3,2},{4,3},{5,4},{6,5},{7,6},{8,7},{9,8},{10,9},{11,1... | collective-permute-start | bytes 32264 | tf_op jit(solution)/shard_map/ppermute | solution.py:29
  299.6 255.0 %all-gather.41.cloned.1.call-start = ((), (), s32[]{:S(2)}) async-start(), calls=%async_computation.8 | async-start | bytes 12976128 | tf_op jit(solution)/shard_map/all_gather | solution.py:37
  441.9 171.4 %all-gather.43.cloned.1.call-start = ((), (), s32[]{:S(2)}) async-start(), calls=%async_computation.9 | async-start | bytes 2433024 | tf_op jit(solution)/shard_map/all_gather | solution.py:422
  443.6 227.6 %all-gather.45.cloned.1.call-start = ((), (), s32[]{:S(2)}) async-start(), calls=%async_computation.10 | async-start | bytes 5474304 | tf_op jit(solution)/shard_map/all_gather | solution.py:418
  444.2 664.1 %all-gather.51.cloned.1.call-start = ((), (), s32[]{:S(2)}) async-start(), calls=%async_computation.13 | async-start | bytes 2433024 | tf_op jit(solution)/shard_map/all_gather | solution.py:422
  444.8 804.4 %all-gather.49.cloned.1.call-start = ((), (), s32[]{:S(2)}) async-start(), calls=%async_computation.12 | async-start | bytes 12976128 | tf_op jit(solution)/shard_map/all_gather | solution.py:37
  498.9 236.8 %copy-start.191 = (f32[1792]{0:T(1024)}, f32[1792]{0:T(1024)S(1)}, u32[]{:S(2)}) copy-start(f32[1792]{0:T(1024)S(1)} %get-tuple-element.6993) | copy-start | bytes 21508
  498.9 236.8 %copy-start.193 = (f32[1792]{0:T(1024)}, f32[1792]{0:T(1024)S(1)}, u32[]{:S(2)}) copy-start(f32[1792]{0:T(1024)S(1)} %get-tuple-element.6994) | copy-start | bytes 21508
  498.9 236.8 %copy-start.195 = (f32[1792]{0:T(1024)}, f32[1792]{0:T(1024)S(1)}, u32[]{:S(2)}) copy-start(f32[1792]{0:T(1024)S(1)} %get-tuple-element.6995) | copy-start | bytes 21508
  505.1 108.2 %copy-start.127 = (f32[1536]{0:T(1024)}, f32[1536]{0:T(1024)S(1)}, u32[]{:S(2)}) copy-start(f32[1536]{0:T(1024)S(1)} %convert_element_type.550) | copy-start | bytes 18436
  505.1 166.1 %copy-start.114 = (f32[768]{0:T(1024)}, f32[768]{0:T(1024)S(1)}, u32[]{:S(2)}) copy-start(f32[768]{0:T(1024)S(1)} %convert_element_type.551) | copy-start | bytes 9220
  684.1 50.6 %collective-permute-start.2 = (bf16[3,1792]{0,1:T(8,128)(2,1)}, bf16[3,1792]{0,1:T(8,128)(2,1)S(1)}, u32[]{:S(2)}, u32[]{:S(2)}) collective-permute-start(bf16[3,1792]{0,1:T(8,128)(2,1)} %get-tuple-element.7885), channel_id=1, source_target_pairs={{0,1},{1,2},{2,3},{3,4},{4,5},{5,6},{6,7},{7,8},{8,9},{9,10},{10,1... | collective-permute-start | bytes 32264 | tf_op jit(solution)/shard_map/ppermute | solution.py:26
  686.3 48.4 %collective-permute-start.3 = (bf16[3,1792]{0,1:T(8,128)(2,1)}, bf16[3,1792]{0,1:T(8,128)(2,1)S(1)}, u32[]{:S(2)}, u32[]{:S(2)}) collective-permute-start(bf16[3,1792]{0,1:T(8,128)(2,1)} %get-tuple-element.7886), channel_id=1, source_target_pairs={{1,0},{2,1},{3,2},{4,3},{5,4},{6,5},{7,6},{8,7},{9,8},{10,9},{11,1... | collective-permute-start | bytes 32264 | tf_op jit(solution)/shard_map/ppermute | solution.py:29
  886.5 685.5 %all-gather.47.cloned.1.call-start = ((), (), s32[]{:S(2)}) async-start(), calls=%async_computation.11 | async-start | bytes 12976128 | tf_op jit(solution)/shard_map/all_gather | solution.py:37
  1249.1 857.3 %all-gather.55.cloned.1.call-start = ((), (), s32[]{:S(2)}) async-start(), calls=%async_computation.15 | async-start | bytes 12976128 | tf_op jit(solution)/shard_map/all_gather | solution.py:63
  1869.0 430.0 %all-gather.53.cloned.1.call-start = ((), (), s32[]{:S(2)}) async-start(), calls=%async_computation.14 | async-start | bytes 12976128 | tf_op jit(solution)/shard_map/all_gather | solution.py:63
  2106.4 619.5 %all-gather.59.cloned.1.call-start = ((), (), s32[]{:S(2)}) async-start(), calls=%async_computation.17 | async-start | bytes 12976128 | tf_op jit(solution)/shard_map/all_gather | solution.py:63
  2574.0 5.4 collective-permute-start.4
  2575.3 5.4 collective-permute-start.5
  2621.8 287.0 %all-gather.57.cloned.1.call-start = ((), (), s32[]{:S(2)}) async-start(), calls=%async_computation.16 | async-start | bytes 12976128 | tf_op jit(solution)/shard_map/all_gather | solution.py:63
  2624.9 626.1 %reduce-scatter.13.cloned.1.call-start = ((), (), s32[]{:S(2)}) async-start(), calls=%async_computation.5 | async-start | bytes 4866048 | tf_op jit(solution)/shard_map/reduce_scatter | solution.py:450
  2633.4 617.6 %reduce-scatter.11.cloned.1.call-start = ((), (), s32[]{:S(2)}) async-start(), calls=%async_computation.4 | async-start | bytes 4866048 | tf_op jit(solution)/shard_map/reduce_scatter | solution.py:450
  2659.7 671.5 %all-reduce.33.cloned.1.call-start = ((), (), s32[]{:S(2)}) async-start(), calls=%async_computation.20 | async-start | bytes 319488
  2972.5 178.4 %copy-start.90 = (f32[384,24]{0,1:T(8,128)S(1)}, f32[384,24]{0,1:T(8,128)}, u32[]{:S(2)}) copy-start(f32[384,24]{0,1:T(8,128)} %copy-done.88) | copy-start | bytes 110596
  2972.5 178.4 %copy-start.242 = (f32[24]{0:T(128)S(1)}, f32[24]{0:T(128)}, u32[]{:S(2)}) copy-start(f32[24]{0:T(128)} %get-tuple-element.7911) | copy-start | bytes 292
  3179.0 5.4 collective-permute-start.6
  3180.5 4.6 collective-permute-start.7
  3197.2 284.1 %reduce-scatter.17.cloned.1.call-start = ((), (), s32[]{:S(2)}) async-start(), calls=%async_computation.19 | async-start | bytes 10948608
  3205.7 423.5 %reduce-scatter.15.cloned.1.call-start = ((), (), s32[]{:S(2)}) async-start(), calls=%async_computation.18 | async-start | bytes 10948608
  (323 other events, 3706.3 us)
Sparse Core Ops, SparseCore 0:
  11.5 71.5 all-gather.36
  299.7 97.6 all-gather.38
  442.0 103.0 all-gather.40
  548.5 55.4 all-gather.42
  606.8 64.4 all-gather.44
  674.0 56.6 all-gather.50
  886.6 97.0 all-gather.48
  1249.2 97.0 all-gather.46
  1869.1 96.8 all-gather.54
  2106.5 96.7 all-gather.52
  2621.9 103.9 all-gather.58
  2729.2 94.2 all-gather.56
  2829.0 105.2 reduce-scatter.12
  2940.5 106.0 reduce-scatter.10
  3197.3 133.9 all-reduce.32
  3338.3 142.9 reduce-scatter.16
  3488.3 140.8 reduce-scatter.14
where the time goes:
time: 3700 us; the launch traced here: 3640 us
  local copies, waits for them, and re-layouts  1570 us (42%)
  other arithmetic  742 us (20%)
  matrix products  548 us (15%)
  waiting for transfers between devices  489 us (13%)
  blocking collectives  216 us (6%)
  loops' own time  41.3 us (1%)
    dynamic_update_slice x240, local copies, waits for them, and re-layouts, scan_direction(): lax.scan(step_function, (state_in, previous), (blocked(values), blocked(w...  943 us
    unnamed x20, waiting for transfers between devices  367 us
    dot_general x48, matrix products, block_step(): within = jnp.einsum('hts,shp->thp', mixing, inputs, precision=precise)  215 us
    select_n x128, other arithmetic, hop(): return jax.tree.map(lambda a, b: jnp.where(reached, a, b), new, before)  188 us
    another operation x135, local copies, waits for them, and re-layouts  160 us
    unnamed x3, blocking collectives  125 us
    dot_general x48, matrix products, block_step(): jnp.einsum('sh,shp,sn->hpn', trailing, inputs, writes, precision=precise)  111 us
    all_gather x2, blocking collectives, shards(): lax.all_gather(conv_w[layer_index], 'seq', axis=0, tiled=True)  90.9 us
  transfers between devices with their start and end apart: 25, of which 7 were waited for; matrix products, arithmetic and copies ran while one was open for 58% of the time, Pallas kernels for 0%

commit v1 on v0

v1 whole, which is shorter than its diff:
```python
import functools

import jax
import jax.numpy as jnp
from jax import lax
from jax.experimental import pallas as pl
from jax.experimental.pallas import tpu as pltpu
from jax.sharding import PartitionSpec as P

HEADS = 24
HEAD = 64
STATE = 64
CONV = 4
SPAN = 128
LAYERS = 2
NSEQ = 8
INNER = 1536
CONVW = 1792
ROWS = 1920
TILE = 256
LANES = 128
RIM = 8
epsilon = 1e-05
bf16 = jnp.bfloat16
f32 = jnp.float32
AXIS = "seq"
PLANE = 4
VMEM_LIMIT = 56 * 1024 * 1024

NN = (((1,), (0,)), ((), ()))
NT = (((1,), (1,)), ((), ()))
TN = (((0,), (0,)), ((), ()))


def dot(a, b, dims=NN):
    return lax.dot_general(a, b, dims, preferred_element_type=f32)


def dot_exact(a, b, dims=NN):
    return lax.dot_general(
        a, b, dims, precision=lax.Precision.HIGHEST, preferred_element_type=f32
    )


def sigmoid(v):
    return 1.0 / (1.0 + jnp.exp(-v))


def softplus(v):
    return jnp.maximum(v, 0.0) + jnp.log1p(jnp.exp(-jnp.abs(v)))


def segment(pos, scalars):
    count = jnp.zeros(pos.shape, jnp.int32) - 1
    for j in range(NSEQ + 1):
        count = count + jnp.where(scalars[2 + j] <= pos, 1, 0)
    count = jnp.where(pos < 0, -1, count)
    return jnp.where(pos >= scalars[1], -2, count)


def iota(shape, axis):
    return lax.broadcasted_iota(jnp.int32, shape, axis)


def spread(coef, onehot):
    high = coef.astype(bf16)
    low = (coef - high.astype(f32)).astype(bf16)
    return dot(jnp.concatenate([high, low], axis=1), onehot)


def gather_heads(values, onehot):
    return dot(values.astype(bf16), onehot[:LANES], NT)


def chunk_marks(scalars, c):
    start = scalars[0] + c * SPAN
    col = segment(start + iota((SPAN, LANES), 0), scalars)
    row = segment(start + iota((1, SPAN), 1), scalars)
    spot = jnp.zeros((1, LANES), jnp.int32) + start
    return (
        col,
        row,
        segment(spot - 1, scalars),
        segment(spot, scalars),
        segment(spot + SPAN - 1, scalars),
        segment(spot + SPAN, scalars),
    )


def edge_weights(kum, total, marks):
    col, _, before, first, last, after = marks
    ahead = iota((SPAN, LANES), 1) < HEADS
    ahead_row = iota((1, LANES), 1) < HEADS
    from_start = jnp.exp(kum)
    to_end = jnp.exp(total - kum)
    near = jnp.where(ahead_row, before, after)
    far = jnp.where(ahead_row, last, first)
    enter = jnp.where(col == near, jnp.where(ahead, from_start, to_end), 0.0)
    leave = jnp.where(col == far, jnp.where(ahead, to_end, from_start), 0.0)
    passing = jnp.where(far == near, jnp.exp(total), 0.0)
    return enter, leave, passing


def chunk_total(kum_ref, la_row, c):
    last = kum_ref[pl.ds(c * SPAN + SPAN - 8, 8), :][7:8, :]
    ahead = iota((1, LANES), 1) < HEADS
    return jnp.where(ahead, last, last + la_row)


def rows8(parts):
    top = jnp.concatenate(parts, axis=0)
    return jnp.concatenate([top, jnp.zeros((8 - top.shape[0], top.shape[1]), top.dtype)], axis=0)


def state_slices(scalars, which, other, bundle, keep_ref, send_ref):
    half = STATE // 2
    for index, ref in ((which, keep_ref), (other, send_ref)):
        for part, state in enumerate(bundle[:2]):
            ref[pl.ds(part * half, half), :] = state[pl.ds(pl.multiple_of(index * half, half), half), :].astype(ref.dtype)
        ref[pl.ds(2 * half, 8), :] = bundle[2].astype(ref.dtype)


def enter_kernel(
    scalars,
    h_ref,
    low_ref,
    high_ref,
    gain_ref,
    w_ref,
    taps_ref,
    head_ref,
    hotf_ref,
    hotr_ref,
    xn_ref,
    rows_ref,
    act_ref,
    dsl_ref,
    dt_ref,
    kum_ref,
    sig_ref,
    tot_ref,
    loc_ref,
    keep_ref,
    send_ref,
    ext_ref,
    lab_ref,
    shift_ref,
    la_ref,
    dev_ref,
):
    extent = h_ref.shape[0]
    wide = extent + 2 * RIM

    def normed(h):
        scale = lax.rsqrt(jnp.mean(h * h, axis=1, keepdims=True) + epsilon)
        return (h * scale * gain_ref[...]).astype(bf16)

    own = normed(h_ref[...])
    xn_ref[...] = own
    ext_ref[pl.ds(0, RIM), :] = normed(low_ref[...])
    ext_ref[pl.ds(RIM, extent), :] = own
    ext_ref[pl.ds(RIM + extent, RIM), :] = normed(high_ref[...])
    lab_ref[...] = segment(scalars[0] - RIM + iota((wide, LANES), 0), scalars)
    lab = lab_ref[pl.ds(RIM, extent), :]
    valid = jnp.where(scalars[0] + iota((extent, LANES), 0) < scalars[2 + NSEQ], 1.0, 0.0)
    valid2 = jnp.concatenate([valid, valid], axis=1)
    masks = []
    for k in range(2 * CONV - 1):
        same = jnp.where(lab_ref[pl.ds(RIM + k - CONV + 1, extent), :] == lab, 1.0, 0.0)
        masks.append(jnp.concatenate([same, same], axis=1))

    def tile(j, carry):
        at = pl.ds(pl.multiple_of(j * TILE, TILE), TILE)
        rows = dot(ext_ref[...], w_ref[:, at]).astype(bf16)
        rows_ref[:, at] = rows
        shift_ref[...] = rows.astype(f32)
        taps = taps_ref[:, at]
        pre = jnp.zeros((extent, TILE), f32) + taps[7:8]
        for k in range(2 * CONV - 1):
            moved = shift_ref[pl.ds(RIM + k - CONV + 1, extent), :]
            pre = pre + taps[k : k + 1] * (moved if k == CONV - 1 else moved * masks[k])
        sig = sigmoid(pre)
        act_ref[:, at] = (pre * sig * valid2).astype(bf16)
        dsl_ref[:, at] = (sig * (1.0 + pre * (1.0 - sig)) * valid2).astype(bf16)
        return carry

    lax.fori_loop(0, CONVW // TILE, tile, 0)
    raw = dot(xn_ref[...], w_ref[:, CONVW:])
    shifted = raw + head_ref[1:2]
    dt = softplus(shifted)
    dt_ref[...] = dt
    sig_ref[...] = sigmoid(shifted)
    la_ref[...] = dt * head_ref[0:1]
    tri = jnp.where(iota((SPAN, SPAN), 0) >= iota((SPAN, SPAN), 1), 1.0, 0.0)
    ahead = iota((SPAN, LANES), 1) < HEADS
    chunks = extent // SPAN
    for c in range(chunks):
        at = pl.ds(c * SPAN, SPAN)
        la = la_ref[at, :]
        full = dot_exact(tri, la)
        total = full[SPAN - 1 :]
        kum = jnp.where(ahead, full, full - la)
        kum_ref[at, :] = kum
        enter, leave, passing = edge_weights(kum, total, chunk_marks(scalars, c))
        coef = leave * dt_ref[at, :]
        tot_ref[pl.ds(c * 8, 8), :] = rows8([total, passing])
        x = act_ref[at, :INNER].astype(f32)
        for d, hot in enumerate((hotf_ref, hotr_ref)):
            scaled = (x * spread(coef, hot[...])).astype(bf16)
            b = act_ref[at, pl.ds(INNER + 2 * STATE * d, STATE)]
            loc_ref[d, c] = dot(b, scaled, TN)
    devices = []
    for d, hot in enumerate((hotf_ref, hotr_ref)):
        state = None
        whole = None
        for c in range(chunks) if d == 0 else reversed(range(chunks)):
            passing = spread(tot_ref[pl.ds(c * 8, 8), :], hot[...])[1:2]
            state = loc_ref[d, c] if state is None else loc_ref[d, c] + passing * state
            whole = passing if whole is None else whole * passing
        dev_ref[d] = state
        devices.append(whole)
    state_slices(
        scalars, scalars[11], 1 - scalars[11], (dev_ref.at[0], dev_ref.at[1], rows8(devices)), keep_ref, send_ref
    )


def within_kernel(scalars, act_ref, dt_ref, kum_ref, skip_ref, y_ref):
    chunks = act_ref.shape[0] // SPAN

    def chunk(c, carry):
        at = pl.ds(pl.multiple_of(c * SPAN, SPAN), SPAN)
        col, row = chunk_marks(scalars, c)[:2]
        t, s = iota((SPAN, SPAN), 0), iota((SPAN, SPAN), 1)
        low = t > s
        bc = act_ref[at, INNER:]
        fore = dot(bc[:, STATE : 2 * STATE], bc[:, :STATE], NT)
        back = dot(bc[:, 3 * STATE :], bc[:, 2 * STATE : 3 * STATE], NT)
        scores = jnp.where(low, fore, back)
        scores = jnp.where((col == row) & (t != s), scores, 0.0)
        kum = kum_ref[at, :]
        kum_t = kum.T
        dt_t = dt_ref[at, :].T
        left = iota((SPAN, LANES), 1) < HEAD
        for pair in range(HEADS // 2):
            mixes = []
            for h in (2 * pair, 2 * pair + 1):
                r = HEADS + h
                gap = jnp.where(
                    low, kum[:, h : h + 1] - kum_t[h : h + 1], kum_t[r : r + 1] - kum[:, r : r + 1]
                )
                step = jnp.where(low, dt_t[h : h + 1], dt_t[r : r + 1])
                mixes.append((jnp.exp(jnp.minimum(gap, 0.0)) * scores * step).astype(bf16))
            lanes = pl.ds(pair * LANES, LANES)
            x = act_ref[at, lanes]
            none = jnp.zeros_like(x)
            stacked = jnp.concatenate([jnp.where(left, x, none), jnp.where(left, none, x)], axis=0)
            y_ref[at, lanes] = dot(jnp.concatenate(mixes, axis=1), stacked) + skip_ref[:, pair * LANES : pair * LANES + LANES] * x.astype(f32)
        return carry

    lax.fori_loop(0, chunks, chunk, 0)


def joined_states(scalars, own_ref, got_ref, d):
    half = STATE // 2
    own = own_ref[pl.ds(d * half, half), :].astype(f32)
    got = got_ref[pl.ds(d * half, half), :].astype(f32)
    first = scalars[11] == 0
    return jnp.concatenate([jnp.where(first, own, got), jnp.where(first, got, own)], axis=0)


def leave_kernel(
    scalars,
    y_in_ref,
    gate_ref,
    act_ref,
    kum_ref,
    tot_ref,
    loc_ref,
    own_ref,
    got_ref,
    gain_ref,
    w_ref,
    h_ref,
    hotf_ref,
    hotr_ref,
    h_out_ref,
    y_ref,
    sin_ref,
):
    extent = h_ref.shape[0]
    chunks = extent // SPAN
    hots = (hotf_ref, hotr_ref)
    for d in range(2):
        state = joined_states(scalars, own_ref, got_ref, d)
        for c in range(chunks) if d == 0 else reversed(range(chunks)):
            sin_ref[d, c] = state.astype(bf16)
            passing = spread(tot_ref[pl.ds(c * 8, 8), :], hots[d][...])[1:2]
            state = loc_ref[d, c] + passing * state
    for c in range(chunks):
        at = pl.ds(c * SPAN, SPAN)
        enter, _, _ = edge_weights(kum_ref[at, :], tot_ref[c * 8 : c * 8 + 1, :], chunk_marks(scalars, c))
        y = y_in_ref[at, :]
        for d in range(2):
            reads = act_ref[at, pl.ds(INNER + 2 * STATE * d, 2 * STATE)][:, STATE:]
            y = y + dot(reads, sin_ref[d, c]) * spread(enter, hots[d][...])
        y_ref[at, :] = y
        gate = gate_ref[at, :]
        m = y * (gate * sigmoid(gate))
        scale = lax.rsqrt(gather_heads(m * m, hotf_ref[...]) * (1.0 / HEAD) + epsilon)
        out = (m * spread(scale, hotf_ref[...]) * gain_ref[...]).astype(bf16)
        h_out_ref[at, :] = h_ref[at, :] + dot(out, w_ref[...])


def gate_kernel(
    scalars,
    g_ref,
    w_ref,
    y_ref,
    gate_ref,
    gain_ref,
    act_ref,
    kum_ref,
    tot_ref,
    hotf_ref,
    hotr_ref,
    gb_ref,
    yn_ref,
    dy_ref,
    dgate_ref,
    sums_ref,
    loc_ref,
    keep_ref,
    send_ref,
    dev_ref,
):
    extent = g_ref.shape[0]
    chunks = extent // SPAN
    hots = (hotf_ref, hotr_ref)
    gain_sum = jnp.zeros((1, INNER), f32)
    skip_sum = jnp.zeros((1, INNER), f32)
    for c in range(chunks):
        at = pl.ds(c * SPAN, SPAN)
        gb = g_ref[at, :].astype(bf16)
        gb_ref[at, :] = gb
        dyn = dot(gb, w_ref[...], NT)
        y = y_ref[at, :]
        gate = gate_ref[at, :]
        sig = sigmoid(gate)
        silu = gate * sig
        m = y * silu
        scale_h = lax.rsqrt(gather_heads(m * m, hotf_ref[...]) * (1.0 / HEAD) + epsilon)
        scale = spread(scale_h, hotf_ref[...])
        normed = m * scale
        yn_ref[at, :] = (normed * gain_ref[...]).astype(bf16)
        gain_sum = gain_sum + jnp.sum(dyn * normed, axis=0, keepdims=True)
        q = dyn * gain_ref[...]
        mean = gather_heads(q * m, hotf_ref[...]) * (1.0 / HEAD)
        dm = scale * q - m * spread(mean * scale_h * scale_h * scale_h, hotf_ref[...])
        dy = dm * silu
        dyb = dy.astype(bf16)
        dy_ref[at, :] = dyb
        dgate_ref[at, :] = (dm * y * sig * (1.0 + gate * (1.0 - sig))).astype(bf16)
        skip_sum = skip_sum + jnp.sum(dy * act_ref[at, :INNER].astype(f32), axis=0, keepdims=True)
        enter, _, _ = edge_weights(kum_ref[at, :], tot_ref[c * 8 : c * 8 + 1, :], chunk_marks(scalars, c))
        for d in range(2):
            reads = act_ref[at, pl.ds(INNER + 2 * STATE * d, 2 * STATE)][:, STATE:]
            loc_ref[d, c] = dot(reads, (dy * spread(enter, hots[d][...])).astype(bf16), TN)
    sums_ref[...] = rows8([gain_sum, skip_sum])
    devices = []
    for d in range(2):
        state = None
        whole = None
        for c in range(chunks) if d == 1 else reversed(range(chunks)):
            passing = spread(tot_ref[pl.ds(c * 8, 8), :], hots[d][...])[1:2]
            state = loc_ref[d, c] if state is None else loc_ref[d, c] + passing * state
            whole = passing if whole is None else whole * passing
        dev_ref[d] = state
        devices.append(whole)
    state_slices(
        scalars,
        scalars[11],
        1 - scalars[11],
        (dev_ref.at[1], dev_ref.at[0], rows8([devices[1], devices[0]])),
        keep_ref,
        send_ref,
    )


def within_back_kernel(scalars, act_ref, dt_ref, kum_ref, dy_ref, skip_ref, dx_ref, dbc_ref, ddt_ref, dk_ref):
    chunks = act_ref.shape[0] // SPAN

    def chunk(c, carry):
        at = pl.ds(pl.multiple_of(c * SPAN, SPAN), SPAN)
        col, row = chunk_marks(scalars, c)[:2]
        s, t = iota((SPAN, SPAN), 0), iota((SPAN, SPAN), 1)
        low = t > s
        bc = act_ref[at, INNER:]
        b_f, c_f = bc[:, :STATE], bc[:, STATE : 2 * STATE]
        b_r, c_r = bc[:, 2 * STATE : 3 * STATE], bc[:, 3 * STATE :]
        joined = (col == row) & (t != s)
        scores = jnp.where(joined, jnp.where(low, dot(b_f, c_f, NT), dot(b_r, c_r, NT)), 0.0)
        kum = kum_ref[at, :]
        kum_t = kum.T
        dt = dt_ref[at, :]
        lane = iota((SPAN, LANES), 1)
        sub = iota((LANES, SPAN), 0)
        left = lane < HEAD
        dscore = jnp.zeros((SPAN, SPAN), f32)
        ddt = jnp.zeros((SPAN, LANES), f32)
        dk_t = jnp.zeros((LANES, SPAN), f32)
        for pair in range(HEADS // 2):
            lanes = pl.ds(pair * LANES, LANES)
            x = act_ref[at, lanes]
            dy = dy_ref[at, lanes]
            none = jnp.zeros_like(x)
            dmix = dot(
                jnp.concatenate([jnp.where(left, x, none), jnp.where(left, none, x)], axis=0), dy, NT
            )
            mixes = []
            for i in range(2):
                h = 2 * pair + i
                r = HEADS + h
                gap = jnp.where(
                    low, kum_t[h : h + 1] - kum[:, h : h + 1], kum[:, r : r + 1] - kum_t[r : r + 1]
                )
                step = jnp.where(low, dt[:, h : h + 1], dt[:, r : r + 1])
                decay = jnp.exp(jnp.minimum(gap, 0.0))
                weight = decay * scores
                mixes.append((weight * step).astype(bf16))
                dw = dmix[i * SPAN : (i + 1) * SPAN]
                dscore = dscore + dw * (decay * step)
                p = dw * weight
                p_low = jnp.where(low, p, 0.0)
                p_up = p - p_low
                ddt_f = jnp.sum(p_low, axis=1, keepdims=True)
                ddt_r = jnp.sum(p_up, axis=1, keepdims=True)
                ddt = jnp.where(lane == h, ddt_f, jnp.where(lane == r, ddt_r, ddt))
                rsum_f = jnp.sum(p_low * step, axis=0, keepdims=True)
                rsum_r = jnp.sum(p_up * step, axis=0, keepdims=True)
                dk_t = jnp.where(sub == h, rsum_f, jnp.where(sub == r, -rsum_r, dk_t))
            stacked = jnp.concatenate([jnp.where(left, dy, none), jnp.where(left, none, dy)], axis=0)
            dx_ref[at, lanes] = dot(jnp.concatenate(mixes, axis=1), stacked) + skip_ref[:, pair * LANES : pair * LANES + LANES] * dy.astype(f32)
        ddt_ref[at, :] = ddt
        dk_ref[at, :] = dk_t.T + jnp.where(lane < HEADS, -1.0, 1.0) * ddt * dt
        d_low = jnp.where(joined & low, dscore, 0.0).astype(bf16)
        d_up = jnp.where(joined & jnp.logical_not(low), dscore, 0.0).astype(bf16)
        dbc_ref[at, :] = jnp.concatenate(
            [dot(d_low, c_f), dot(d_low, b_f, TN), dot(d_up, c_r), dot(d_up, b_r, TN)], axis=1
        )
        return carry

    lax.fori_loop(0, chunks, chunk, 0)


def across_back_kernel(
    scalars,
    act_ref,
    dt_ref,
    kum_ref,
    sig_ref,
    tot_ref,
    dy_ref,
    dx_ref,
    dbc_ref,
    ddt_ref,
    dk_ref,
    loc_ref,
    sin_ref,
    own_ref,
    got_ref,
    dsl_ref,
    head_ref,
    hotf_ref,
    hotr_ref,
    dpre_ref,
    draw_ref,
    sums_ref,
    sout_ref,
):
    extent = act_ref.shape[0]
    chunks = extent // SPAN
    hots = (hotf_ref, hotr_ref)
    for d in range(2):
        state = joined_states(scalars, own_ref, got_ref, 1 - d)
        for c in range(chunks) if d == 1 else reversed(range(chunks)):
            sout_ref[d, c] = state
            passing = spread(tot_ref[pl.ds(c * 8, 8), :], hots[d][...])[1:2]
            state = loc_ref[d, c] + passing * state
    ahead = iota((SPAN, LANES), 1) < HEADS
    a, b = iota((SPAN, SPAN), 0), iota((SPAN, SPAN), 1)
    rate_sum = jnp.zeros((1, LANES), f32)
    raw_sum = jnp.zeros((1, LANES), f32)
    for c in range(chunks):
        at = pl.ds(c * SPAN, SPAN)
        kum = kum_ref[at, :]
        dt = dt_ref[at, :]
        enter, leave, passing = edge_weights(kum, tot_ref[c * 8 : c * 8 + 1, :], chunk_marks(scalars, c))
        x = act_ref[at, :INNER].astype(f32)
        dy = dy_ref[at, :].astype(f32)
        dx = dx_ref[at, :]
        dbc = []
        ins, outs, thr = [], [], []
        for d in range(2):
            hot = hots[d][...]
            writes = act_ref[at, pl.ds(INNER + 2 * STATE * d, STATE)]
            reads = act_ref[at, pl.ds(INNER + 2 * STATE * d, 2 * STATE)][:, STATE:]
            s_in = sin_ref[d, c]
            s_out = sout_ref[d, c]
            s_out_b = s_out.astype(bf16)
            leave_w = spread(leave * dt, hot)
            dc = dot((dy * spread(enter, hot)).astype(bf16), s_in, NT)
            db = dot((x * leave_w).astype(bf16), s_out_b, NT)
            seen = dot(reads, s_in)
            given = dot(writes, s_out_b)
            dx = dx + given * leave_w
            ins.append(gather_heads(dy * seen, hot))
            outs.append(gather_heads(x * given, hot))
            thr.append(gather_heads(rows8([jnp.sum(s_in.astype(f32) * s_out, axis=0, keepdims=True)]), hot)[0:1])
            dbc += [db, dc]
        d_in = (ins[0] + ins[1]) * enter
        d_out = (outs[0] + outs[1]) * leave
        through = (thr[0] + thr[1]) * passing
        dt_out = d_out * dt
        dk = dk_ref[at, :]
        later = jnp.where(ahead, dk + d_in, 0.0)
        earlier = jnp.where(ahead, dt_out, 0.0)
        dla_f = dot_exact(jnp.where(b >= a, 1.0, 0.0), later) + dot_exact(jnp.where(b < a, 1.0, 0.0), earlier)
        upto = jnp.where(ahead, 0.0, d_in)
        beyond = jnp.where(ahead, 0.0, dt_out + dk)
        dla_r = dot_exact(jnp.where(b <= a, 1.0, 0.0), upto) + dot_exact(jnp.where(b > a, 1.0, 0.0), beyond)
        dla = dla_f + dla_r + through
        neg_rate = head_ref[0:1]
        ddt = ddt_ref[at, :] + d_out + neg_rate * dla
        draw = ddt * sig_ref[at, :]
        rate_sum = rate_sum + jnp.sum(dla * (dt * neg_rate), axis=0, keepdims=True)
        raw_sum = raw_sum + jnp.sum(draw, axis=0, keepdims=True)
        draw_ref[at, :] = jnp.where(iota((SPAN, LANES), 1) < 2 * HEADS, draw, 0.0).astype(bf16)
        dpre_ref[at, :INNER] = (dx * dsl_ref[at, :INNER].astype(f32)).astype(bf16)
        dbc = dbc_ref[at, :] + jnp.concatenate(dbc, axis=1)
        dpre_ref[at, INNER:] = (dbc * dsl_ref[at, INNER:].astype(f32)).astype(bf16)
    sums_ref[...] = rows8([rate_sum, raw_sum])


def taps_kernel(scalars, rows_ref, dpre_ref, dtaps_ref, shift_ref, lab_ref):
    extent = dpre_ref.shape[0]
    wide = extent + 2 * RIM
    lab_ref[...] = segment(scalars[0] - RIM + iota((wide, LANES), 0), scalars)
    lab = lab_ref[pl.ds(RIM, extent), :]
    masks = []
    for k in range(2 * CONV - 1):
        same = jnp.where(lab_ref[pl.ds(RIM + k - CONV + 1, extent), :] == lab, 1.0, 0.0)
        masks.append(jnp.concatenate([same, same], axis=1))

    def tile(j, carry):
        at = pl.ds(pl.multiple_of(j * TILE, TILE), TILE)
        dpre = dpre_ref[:, at].astype(f32)
        shift_ref[...] = rows_ref[:, at].astype(f32)
        parts = []
        for k in range(2 * CONV - 1):
            moved = shift_ref[pl.ds(RIM + k - CONV + 1, extent), :]
            parts.append(jnp.sum(dpre * (moved if k == CONV - 1 else moved * masks[k]), axis=0, keepdims=True))
        parts.append(jnp.sum(dpre, axis=0, keepdims=True))
        dtaps_ref[:, at] = jnp.concatenate(parts, axis=0)
        return carry

    lax.fori_loop(0, CONVW // TILE, tile, 0)


def proj_back_kernel(
    scalars, dpre_ref, low_ref, high_ref, taps_ref, draw_ref, xn_ref, dproj_ref, gw_ref, shift_ref, lab_ref
):
    extent = dpre_ref.shape[0]
    wide = extent + 2 * RIM
    lab_ref[...] = segment(scalars[0] - RIM + iota((wide, LANES), 0), scalars)
    lab = lab_ref[pl.ds(RIM, extent), :]
    masks = []
    for k in range(2 * CONV - 1):
        same = jnp.where(lab_ref[pl.ds(RIM + CONV - 1 - k, extent), :] == lab, 1.0, 0.0)
        masks.append(jnp.concatenate([same, same], axis=1))

    def tile(j, carry):
        at = pl.ds(pl.multiple_of(j * TILE, TILE), TILE)
        shift_ref[pl.ds(0, RIM), :] = low_ref[:, at].astype(f32)
        shift_ref[pl.ds(RIM, extent), :] = dpre_ref[:, at].astype(f32)
        shift_ref[pl.ds(RIM + extent, RIM), :] = high_ref[:, at].astype(f32)
        taps = taps_ref[:, at]
        drows = jnp.zeros((extent, TILE), f32)
        for k in range(2 * CONV - 1):
            moved = shift_ref[pl.ds(RIM + CONV - 1 - k, extent), :]
            drows = drows + taps[k : k + 1] * (moved if k == CONV - 1 else moved * masks[k])
        drows = drows.astype(bf16)
        dproj_ref[:, at] = drows
        gw_ref[:, at] = dot(xn_ref[...], drows, TN).astype(bf16)
        return carry

    lax.fori_loop(0, CONVW // TILE, tile, 0)
    draw = draw_ref[...]
    dproj_ref[:, CONVW:] = draw
    gw_ref[:, CONVW:] = dot(xn_ref[...], draw, TN).astype(bf16)


def norm_back_kernel(dproj_ref, dgate_ref, wr_ref, wg_ref, h_ref, gain_ref, g_ref, g_out_ref, sums_ref):
    dxn = dot(dproj_ref[...], wr_ref[...], NT) + dot(dgate_ref[...], wg_ref[...], NT)
    h = h_ref[...]
    factor = lax.rsqrt(jnp.mean(h * h, axis=1, keepdims=True) + epsilon)
    hr = h * factor
    sums_ref[...] = rows8([jnp.sum(dxn * hr, axis=0, keepdims=True)])
    q = dxn * gain_ref[...]
    g_out_ref[...] = (
        g_ref[...] + factor * q - hr * (factor * factor) * jnp.mean(q * h, axis=1, keepdims=True)
    )


def chip_kernel(scalars, keep_ref, got_ref, send_ref, own_ref):
    half = STATE // 2
    part = half // PLANE
    first = scalars[11] == 0
    keep = keep_ref[...].astype(f32)
    got = got_ref[...].astype(f32)
    early = jnp.where(first, keep, got)
    late = jnp.where(first, got, keep)
    d_early, d_late = early[2 * half : 2 * half + 8], late[2 * half : 2 * half + 8]
    fore = late[:half] + d_late[0:1] * early[:half]
    back = early[half : 2 * half] + d_early[1:2] * late[half : 2 * half]
    both = (d_early * d_late).astype(bf16)
    for j in range(PLANE):
        rows = slice(j * part, (j + 1) * part)
        send_ref[j, 0:part] = fore[rows].astype(bf16)
        send_ref[j, part : 2 * part] = back[rows].astype(bf16)
        send_ref[j, 2 * part :] = both
    own_ref[0:half] = early[:half]
    own_ref[half : 2 * half] = late[half : 2 * half]
    own_ref[2 * half :] = rows8([d_early[0:1], d_late[1:2]])


def plane_kernel(scalars, mine_ref, a_ref, b_ref, c_ref, send_ref, pre_ref, order_ref):
    part = STATE // 2 // PLANE
    chip = scalars[12]
    for m, ref in enumerate((mine_ref, a_ref, b_ref, c_ref)):
        order_ref[chip ^ m] = ref[...].astype(f32)
    fore = jnp.zeros((part, INNER), f32)
    back = jnp.zeros((part, INNER), f32)
    d_fore = jnp.ones((1, INNER), f32)
    d_back = jnp.ones((1, INNER), f32)
    for k in range(PLANE):
        j = k
        pre_ref[0, j] = fore
        pre_ref[2, j] = jnp.broadcast_to(d_fore, (part, INNER))
        dec = order_ref[j, 2 * part :][0:1]
        fore = order_ref[j, 0:part] + dec * fore
        d_fore = d_fore * dec
        j = PLANE - 1 - k
        pre_ref[1, j] = back
        pre_ref[3, j] = jnp.broadcast_to(d_back, (part, INNER))
        dec = order_ref[j, 2 * part :][1:2]
        back = order_ref[j, part : 2 * part] + dec * back
        d_back = d_back * dec
    decays = rows8([d_fore, d_back])
    send_ref[0] = jnp.concatenate([fore, decays], axis=0).astype(bf16)
    send_ref[1] = jnp.concatenate([back, decays], axis=0).astype(bf16)


def column_kernel(groups, scalars, pre_ref, *refs):
    got = refs[: groups - 1]
    out_ref, order_ref = refs[groups - 1 :]
    part = STATE // 2 // PLANE
    z = scalars[13]
    order_ref[z] = jnp.zeros((part + 8, INNER), f32)
    for m in range(1, groups):
        order_ref[z ^ m] = got[m - 1][...].astype(f32)
    fore = jnp.zeros((part, INNER), f32)
    back = jnp.zeros((part, INNER), f32)
    for k in range(groups):
        fore = jnp.where(k < z, order_ref[k, 0:part] + order_ref[k, part:][0:1] * fore, fore)
        j = groups - 1 - k
        back = jnp.where(j > z, order_ref[j, 0:part] + order_ref[j, part:][1:2] * back, back)
    for j in range(PLANE):
        out_ref[j, 0:part] = (pre_ref[0, j] + pre_ref[2, j] * fore).astype(bf16)
        out_ref[j, part:] = (pre_ref[1, j] + pre_ref[3, j] * back).astype(bf16)


def back_kernel(scalars, own_ref, mine_ref, a_ref, b_ref, c_ref, keep_ref, send_ref, order_ref):
    half = STATE // 2
    part = half // PLANE
    chip = scalars[12]
    for m, ref in enumerate((mine_ref, a_ref, b_ref, c_ref)):
        order_ref[chip ^ m] = ref[...].astype(f32)
    fore = jnp.concatenate([order_ref[j, 0:part] for j in range(PLANE)], axis=0)
    back = jnp.concatenate([order_ref[j, part:] for j in range(PLANE)], axis=0)
    decays = own_ref[2 * half :]
    fore_late = own_ref[0:half] + decays[0:1] * fore
    back_early = own_ref[half : 2 * half] + decays[1:2] * back
    early = jnp.concatenate([fore, back_early], axis=0).astype(bf16)
    late = jnp.concatenate([fore_late, back], axis=0).astype(bf16)
    first = scalars[11] == 0
    keep_ref[...] = jnp.where(first, early, late)
    send_ref[...] = jnp.where(first, late, early)


def whole(shape, dtype):
    return jax.ShapeDtypeStruct(shape, dtype)


def call(kernel, scalars, arrays, outs, scratch=(), flops=0, name=None):
    moved = sum(a.size * a.dtype.itemsize for a in arrays)
    moved += sum(o.size * o.dtype.itemsize for o in outs)
    smem = [pl.BlockSpec(memory_space=pltpu.SMEM)] if scalars is not None else []
    args = ([scalars] if scalars is not None else []) + list(arrays)
    return pl.pallas_call(
        kernel,
        out_shape=tuple(outs),
        in_specs=smem + [pl.BlockSpec(memory_space=pltpu.VMEM)] * len(arrays),
        out_specs=tuple(pl.BlockSpec(memory_space=pltpu.VMEM) for _ in outs),
        scratch_shapes=list(scratch),
        compiler_params=pltpu.CompilerParams(vmem_limit_bytes=VMEM_LIMIT),
        cost_estimate=pl.CostEstimate(flops=flops, bytes_accessed=moved, transcendentals=0),
        name=name,
    )(*args)


def partner(value, mask):
    count = lax.axis_size(AXIS)
    return lax.ppermute(value, AXIS, [(i, i ^ mask) for i in range(count)])


def exchange(scalars, keep, send):
    count = lax.axis_size(AXIS)
    groups = count // (2 * PLANE)
    place = lax.axis_index(AXIS)
    chip, z = (place // 2) % PLANE, place // (2 * PLANE)
    half, part = STATE // 2, STATE // 2 // PLANE
    got = partner(send, 1)
    cut, own = call(
        chip_kernel,
        scalars,
        (keep, got),
        (whole((PLANE, 2 * part + 8, INNER), bf16), whole((2 * half + 8, INNER), f32)),
        name="chip_states",
    )

    def to(chips, m):
        return lax.dynamic_index_in_dim(chips, chip ^ m, 0, False)

    around = [partner(to(cut, m), 2 * m) for m in range(1, PLANE)]
    total, pre = call(
        plane_kernel,
        scalars,
        (to(cut, 0), *around),
        (whole((2, part + 8, INNER), bf16), whole((4, PLANE, part, INNER), f32)),
        [pltpu.VMEM((PLANE, 2 * part + 8, INNER), f32)],
        name="plane_states",
    )
    column = []
    for m in range(1, groups):
        up = (z ^ m) > z
        column.append(partner(jnp.where(up, total[0], total[1]), 2 * PLANE * m))
    (entering,) = call(
        functools.partial(column_kernel, groups),
        scalars,
        (pre, *column),
        (whole((PLANE, 2 * part, INNER), bf16),),
        [pltpu.VMEM((groups, part + 8, INNER), f32)],
        name="column_states",
    )
    around = [partner(to(entering, m), 2 * m) for m in range(1, PLANE)]
    mine, theirs = call(
        back_kernel,
        scalars,
        (own, to(entering, 0), *around),
        (whole((2 * half, INNER), bf16), whole((2 * half, INNER), bf16)),
        [pltpu.VMEM((PLANE, 2 * part, INNER), f32)],
        name="core_states",
    )
    return mine, partner(theirs, 1)


def shares(count):
    groups = count // (2 * PLANE)
    return [core + 2 * p + 2 * PLANE * g for core in range(2) for p in range(PLANE) for g in range(groups)]


def by_owner(place, count):
    groups = count // (2 * PLANE)
    mask = jnp.arange(count, dtype=jnp.int32) ^ place
    position = (mask % 2) * (PLANE * groups) + ((mask // 2) % PLANE) * groups + mask // (2 * PLANE)
    return position, jnp.array(shares(count), jnp.int32) ^ place


def gathered(block):
    count = lax.axis_size(AXIS)
    groups = count // (2 * PLANE)
    part = jnp.stack([block] + [partner(block, 2 * PLANE * m) for m in range(1, groups)])
    part = jnp.concatenate([part] + [partner(part, 2 * m) for m in range(1, PLANE)], axis=0)
    return jnp.concatenate([part, partner(part, 1)], axis=0)


def summed(blocks):
    count = lax.axis_size(AXIS)
    groups = count // (2 * PLANE)
    half = count // 2
    dtype = blocks.dtype
    kept = (blocks[:half].astype(f32) + partner(blocks[half:], 1).astype(f32)).astype(dtype)
    total = kept[:groups].astype(f32)
    for m in range(1, PLANE):
        total = total + partner(kept[m * groups : (m + 1) * groups], 2 * m).astype(f32)
    kept = total.astype(dtype)
    total = kept[0].astype(f32)
    for m in range(1, groups):
        total = total + partner(kept[m], 2 * PLANE * m).astype(f32)
    return total


def everywhere(value):
    count = lax.axis_size(AXIS)
    groups = count // (2 * PLANE)
    value = value + partner(value, 1)
    value = value + sum(partner(value, 2 * m) for m in range(1, PLANE))
    return value + sum(partner(value, 2 * PLANE * m) for m in range(1, groups))


def ordered(stack, position):
    taken = jnp.take(stack, position, axis=0)
    return taken.reshape((taken.shape[0] * taken.shape[1],) + taken.shape[2:])


def rims(block):
    count = lax.axis_size(AXIS)
    length = block.shape[0]
    up = [(i, i + 1) for i in range(count - 1)]
    down = [(i + 1, i) for i in range(count - 1)]
    low = lax.ppermute(block[length - RIM :], AXIS, up)
    high = lax.ppermute(block[:RIM], AXIS, down)
    return low, high


def layer_forward(hidden, weights, scalars, hots):
    extent = hidden.shape[0]
    chunks = extent // SPAN
    low, high = rims(hidden)
    (xn, rows, act, dsl, dt, kum, sig, tot, loc, keep, send) = call(
        enter_kernel,
        scalars,
        (hidden, low, high, weights["gain_in"], weights["w_rows"], weights["taps"], weights["head"], *hots),
        (
            whole((extent, hidden.shape[1]), bf16),
            whole((extent + 2 * RIM, CONVW), bf16),
            whole((extent, CONVW), bf16),
            whole((extent, CONVW), bf16),
            whole((extent, LANES), f32),
            whole((extent, LANES), f32),
            whole((extent, LANES), f32),
            whole((chunks * 8, LANES), f32),
            whole((2, chunks, STATE, INNER), f32),
            whole((STATE + 8, INNER), bf16),
            whole((STATE + 8, INNER), bf16),
        ),
        [
            pltpu.VMEM((extent + 2 * RIM, hidden.shape[1]), bf16),
            pltpu.VMEM((extent + 2 * RIM, LANES), jnp.int32),
            pltpu.VMEM((extent + 2 * RIM, TILE), f32),
            pltpu.VMEM((extent, LANES), f32),
            pltpu.VMEM((2, STATE, INNER), f32),
        ],
        flops=2 * extent * hidden.shape[1] * ROWS,
        name="enter",
    )
    (y_in,) = call(
        within_kernel,
        scalars,
        (act, dt, kum, weights["skip"]),
        (whole((extent, INNER), f32),),
        flops=2 * extent * SPAN * INNER,
        name="within",
    )
    gate = dot(xn, weights["w_gate"])
    own, got = exchange(scalars, keep, send)
    out, y, sin = call(
        leave_kernel,
        scalars,
        (
            y_in,
            gate,
            act,
            kum,
            tot,
            loc,
            own,
            got,
            weights["gain_out"],
            weights["w_out"],
            hidden,
            *hots,
        ),
        (
            whole(hidden.shape, f32),
            whole((extent, INNER), f32),
            whole((2, chunks, STATE, INNER), bf16),
        ),
        flops=2 * extent * hidden.shape[1] * INNER,
        name="leave",
    )
    return out, (hidden, xn, rows, act, dsl, dt, kum, sig, tot, gate, y, sin)


def layer_backward(grad, stored, weights, scalars, hots, order):
    hidden, xn, rows, act, dsl, dt, kum, sig, tot, gate, y, sin = stored
    extent, width = hidden.shape
    chunks = extent // SPAN
    gb, yn, dy, dgate, sums_y, loc, keep, send = call(
        gate_kernel,
        scalars,
        (grad, weights["w_out"], y, gate, weights["gain_out"], act, kum, tot, *hots),
        (
            whole((extent, width), bf16),
            whole((extent, INNER), bf16),
            whole((extent, INNER), bf16),
            whole((extent, INNER), bf16),
            whole((8, INNER), f32),
            whole((2, chunks, STATE, INNER), f32),
            whole((STATE + 8, INNER), bf16),
            whole((STATE + 8, INNER), bf16),
        ),
        [pltpu.VMEM((2, STATE, INNER), f32)],
        flops=2 * extent * width * INNER,
        name="gate_back",
    )
    dx, dbc, ddt, dk = call(
        within_back_kernel,
        scalars,
        (act, dt, kum, dy, weights["skip"]),
        (
            whole((extent, INNER), f32),
            whole((extent, 4 * STATE), f32),
            whole((extent, LANES), f32),
            whole((extent, LANES), f32),
        ),
        flops=4 * extent * SPAN * INNER,
        name="within_back",
    )
    gw_out = dot(yn, gb, TN).astype(bf16)
    gw_gate = dot(xn, dgate, TN).astype(bf16)
    own, got = exchange(scalars, keep, send)
    dpre, draw, sums_h = call(
        across_back_kernel,
        scalars,
        (act, dt, kum, sig, tot, dy, dx, dbc, ddt, dk, loc, sin, own, got, dsl, weights["head"], *hots),
        (whole((extent, CONVW), bf16), whole((extent, LANES), bf16), whole((8, LANES), f32)),
        [pltpu.VMEM((2, chunks, STATE, INNER), f32)],
        flops=8 * extent * STATE * INNER,
        name="across_back",
    )
    low, high = rims(dpre)
    (dtaps,) = call(
        taps_kernel,
        scalars,
        (rows, dpre),
        (whole((8, CONVW), f32),),
        [pltpu.VMEM((extent + 2 * RIM, TILE), f32), pltpu.VMEM((extent + 2 * RIM, LANES), jnp.int32)],
        name="taps_back",
    )
    dproj, gw_rows = call(
        proj_back_kernel,
        scalars,
        (dpre, low, high, weights["taps"], draw, xn),
        (whole((extent, ROWS), bf16), whole((width, ROWS), bf16)),
        [pltpu.VMEM((extent + 2 * RIM, TILE), f32), pltpu.VMEM((extent + 2 * RIM, LANES), jnp.int32)],
        flops=2 * extent * width * ROWS,
        name="proj_back",
    )
    grad_in, sums_d = call(
        norm_back_kernel,
        None,
        (dproj, dgate, weights["w_rows"], weights["w_gate"], hidden, weights["gain_in"], grad),
        (whole((extent, width), f32), whole((8, width), f32)),
        flops=2 * extent * width * (ROWS + INNER),
        name="norm_back",
    )
    return grad_in, (gw_rows, gw_gate, gw_out, dtaps, sums_y, sums_h, sums_d)


def shard_program(tokens, cotangent, offsets, gain_in, w_in, conv_w, conv_b, gain_out, w_out, head_params):
    length, width = tokens.shape
    count = lax.axis_size(AXIS)
    place = lax.axis_index(AXIS)
    scalars = jnp.concatenate(
        [
            jnp.stack([place * length, jnp.int32(count * length)]),
            offsets,
            jnp.stack([place % 2, (place // 2) % PLANE, place // (2 * PLANE)]),
        ]
    ).astype(jnp.int32)
    position, owner = by_owner(place, count)
    k_index = jnp.arange(2 * LANES)[:, None] % LANES
    head_of = jnp.arange(INNER)[None, :] // HEAD
    hots = ((k_index == head_of).astype(bf16), (k_index == head_of + HEADS).astype(bf16))

    cw, gi, go = conv_w.shape[1], gain_in.shape[1], gain_out.shape[1]
    taps_count = 2 * CONV - 1
    small = jnp.concatenate(
        [conv_w.transpose(0, 2, 1).reshape(-1), conv_b.reshape(-1), gain_in.reshape(-1), gain_out.reshape(-1)]
    )
    small_len = small.shape[0]
    small_rows = -(-small_len // (8 * LANES)) * 8
    small = jnp.pad(small, (0, small_rows * LANES - small_len)).reshape(small_rows, LANES)
    small = jnp.take(gathered(small).reshape(count, small_rows * LANES), position, axis=0).astype(f32)
    at = 0

    def taken(*shape):
        nonlocal at
        size = 1
        for n in shape:
            size *= n
        part = small[:, at : at + size].reshape((count,) + shape)
        at += size
        return part

    conv_w_all = taken(LAYERS, taps_count, cw).transpose(1, 2, 0, 3).reshape(LAYERS, taps_count, CONVW)
    conv_b_all = taken(LAYERS, cw).transpose(1, 0, 2).reshape(LAYERS, 1, CONVW)
    gain_in_all = taken(LAYERS, gi).transpose(1, 0, 2).reshape(LAYERS, 1, width)
    gain_out_all = taken(LAYERS, go).transpose(1, 0, 2).reshape(LAYERS, 1, INNER)
    taps_all = jnp.concatenate([conv_w_all, conv_b_all], axis=1)

    layers = []
    for l in range(LAYERS):
        w_rows = jnp.pad(w_in[l, :, INNER:], ((0, 0), (0, ROWS - CONVW - 2 * HEADS)))
        neg_rate = -jnp.exp(head_params[l, 0])
        zero = jnp.zeros((LANES - 2 * HEADS,), f32)
        head = jnp.stack(
            [
                jnp.concatenate([neg_rate, neg_rate, zero]),
                jnp.concatenate([head_params[l, 1], head_params[l, 2], zero]),
            ]
        )
        layers.append(
            dict(
                w_rows=ordered(gathered(w_rows), position),
                w_gate=ordered(gathered(w_in[l, :, :INNER]), position),
                w_out=ordered(gathered(w_out[l]), position),
                taps=taps_all[l],
                gain_in=gain_in_all[l],
                gain_out=gain_out_all[l],
                head=jnp.pad(head, ((0, 6), (0, 0))),
                skip=jnp.repeat(head_params[l, 3], HEAD)[None],
            )
        )
    hidden = tokens.astype(f32)
    stored = []
    for l in range(LAYERS):
        hidden, kept = layer_forward(hidden, layers[l], scalars, hots)
        stored.append(kept)
    result = hidden.astype(bf16)
    grad = cotangent.astype(f32)
    outs = [None] * LAYERS
    heads = [None] * LAYERS
    for l in reversed(range(LAYERS)):
        grad, (gw_rows, gw_gate, gw_out, dtaps, sums_y, sums_h, sums_d) = layer_backward(
            grad, stored[l], layers[l], scalars, hots, owner
        )

        def share(full):
            blocks = full.reshape((count, full.shape[0] // count) + full.shape[1:])
            return summed(jnp.take(blocks, owner, axis=0))

        s_rows, s_gate, s_out = share(gw_rows), share(gw_gate), share(gw_out)
        little = jnp.concatenate(
            [
                dtaps.reshape(8, count, cw).transpose(1, 0, 2).reshape(count, 8 * cw),
                sums_d[0].reshape(count, gi),
                sums_y[0].reshape(count, go),
            ],
            axis=1,
        )
        little_len = little.shape[1]
        little = jnp.pad(little, ((0, 0), (0, -little_len % (8 * LANES)))).reshape(count, -1, LANES)
        little = summed(jnp.take(little, owner, axis=0)).reshape(-1)
        d_taps = little[: 8 * cw].reshape(8, cw)
        outs[l] = (
            little[8 * cw : 8 * cw + gi],
            jnp.concatenate([s_gate, s_rows[:, : CONVW + 2 * HEADS]], axis=1),
            d_taps[:taps_count].T,
            d_taps[taps_count],
            little[8 * cw + gi : 8 * cw + gi + go],
            s_out,
        )
        heads[l] = jnp.stack(
            [
                sums_h[0, :HEADS] + sums_h[0, HEADS : 2 * HEADS],
                sums_h[1, :HEADS],
                sums_h[1, HEADS : 2 * HEADS],
                sums_y[1].reshape(HEADS, HEAD).sum(axis=1),
            ]
        )
    head_total = everywhere(jnp.stack(heads))
    stacked = [jnp.stack([outs[l][member] for l in range(LAYERS)]) for member in range(6)]
    return (result, grad, *stacked, head_total)


def solution(mesh):
    in_specs = (
        P(AXIS, None),
        P(AXIS, None),
        P(),
        P(None, AXIS),
        P(None, AXIS, None),
        P(None, AXIS, None),
        P(None, AXIS),
        P(None, AXIS),
        P(None, AXIS, None),
        P(),
    )
    out_specs = (
        P(AXIS, None),
        P(AXIS, None),
        P(None, AXIS),
        P(None, AXIS, None),
        P(None, AXIS, None),
        P(None, AXIS),
        P(None, AXIS),
        P(None, AXIS, None),
        P(),
    )
    return jax.shard_map(shard_program, mesh=mesh, in_specs=in_specs, out_specs=out_specs, check_vma=False)
```

time: 3700 us -> 845 us (0.23); the launches traced: 3640 us -> 836 us
  local copies, waits for them, and re-layouts: 1570 us -> 155 us
  other arithmetic: 742 us -> 59.5 us
  matrix products: 548 us -> 14.6 us
  waiting for transfers between devices: 489 us -> 173 us
  Pallas kernels: 0 us -> 238 us
  blocking collectives: 216 us -> 0 us
  starting transfers between devices: 13.9 us -> 193 us
  loops' own time: 41.3 us -> 0 us
    dynamic_update_slice x240 -> x0, local copies, waits for them, and re-layouts: 943 us -> none  [scan_direction(): lax.scan(step_function, (state_in, previous), (blocked(values), blocked(w...]
    dot_general x212 -> x6, matrix products: 548 us -> 14.6 us  [dot(): return lax.dot_general(a, b, dims, preferred_element_type=f32)]
    unnamed x20 -> x0, waiting for transfers between devices: 367 us -> none
    pallas_call x0 -> x34, Pallas kernels: none -> 238 us  [call(): pl.pallas_call(kernel, out_shape=tuple(outs), in_specs=smem + [pl.BlockSp...]
    select_n x218 -> x15, other arithmetic: 241 us -> 25.8 us  [the longest x3 12.3 us: ordered(): taken = jnp.take(stack, position, axis=0)]
    ppermute x8 -> x164, starting transfers between devices: 12.6 us -> 193 us  [the longest x156 180 us: partner(): return lax.ppermute(value, AXIS, [(i, i ^ mask) for i in range(count)])]
    another operation x173 -> x16, local copies, waits for them, and re-layouts: 179 us -> 3.44 us  [the longest x2 1.35 us: shard_program(): jnp.repeat(head_params[l, 3], HEAD)[None]]
    ppermute x8 -> x164, waiting for transfers between devices: 2.08 us -> 173 us  [the longest x156 169 us: partner(): return lax.ppermute(value, AXIS, [(i, i ^ mask) for i in range(count)])]
  transfers between devices with their start and end apart: 25 -> 164, of which waited for: 7 -> 65; matrix products, arithmetic and copies ran while one was open for 58% -> 23% of each run, Pallas kernels for 0% -> 14%
where the time goes in v1:
time: 845 us; the launch traced here: 836 us
  Pallas kernels  238 us (28%)
  starting transfers between devices  193 us (23%)
  waiting for transfers between devices  173 us (20%)
  local copies, waits for them, and re-layouts  155 us (18%)
  other arithmetic  59.5 us (7%)
  matrix products  14.6 us (2%)
    pallas_call x34, Pallas kernels, call(): pl.pallas_call(kernel, out_shape=tuple(outs), in_specs=smem + [pl.BlockSp...  238 us
    ppermute x156, starting transfers between devices, partner(): return lax.ppermute(value, AXIS, [(i, i ^ mask) for i in range(count)])  180 us
    ppermute x156, waiting for transfers between devices, partner(): return lax.ppermute(value, AXIS, [(i, i ^ mask) for i in range(count)])  169 us
    unnamed x253, local copies, waits for them, and re-layouts  50.1 us
    gather x6, local copies, waits for them, and re-layouts, ordered(): taken = jnp.take(stack, position, axis=0)  19.3 us
    gather x6, local copies, waits for them, and re-layouts, share(): return summed(jnp.take(blocks, owner, axis=0))  19.2 us
  transfers between devices with their start and end apart: 164, of which 65 were waited for; matrix products, arithmetic and copies ran while one was open for 23% of the time, Pallas kernels for 14%

profile of v1, /device:TPU:0, one launch (start us, length us, event | category | flops | bytes accessed | tf_op | source)
XLA Modules:
  0.0 835.9 jit_solution(11912218547313839326)
XLA Ops:
  118.2 6.0 collective-permute-done.20
  128.1 12.7 %collective-permute-done.46 = bf16[4,24,1920]{2,1,0:T(8,128)(2,1)S(1)} collective-permute-done((bf16[4,24,1920]{2,1,0:T(8,128)(2,1)S(1)}, bf16[4,24,1920]{2,1,0:T(8,128)(2,1)S(1)}, u32[]{:S(2)}, u32[]{:S(2)}) %collective-permute-start.46) | collective-permute-done | bytes 368672 | tf_op jit(solution)/shard_map/ppermute | solution.py:723
  145.7 7.5 collective-permute-done.48
  181.7 5.4 collective-permute-done.39
  214.4 5.2 broadcast_select_fusion.2
  220.3 16.1 %enter.2 = (bf16[384,768]{1,0:T(8,128)(2,1)}, bf16[400,1792]{1,0:T(8,128)(2,1)}, bf16[384,1792]{1,0:T(8,128)(2,1)}, bf16[384,1792]{1,0:T(8,128)(2,1)}, f32[384,1...) custom-call(s32[14]{0:T(128)} %concatenate.106.scalars, ...), custom_call_target="tpu_custom_call" | custom-call | flops 1132462080 | bytes 13995008 | tf_op jit(solution)/shard_map/enter/pallas_call | solution.py:709
  280.3 7.3 within.2.y_in_ref
  293.4 11.0 %leave.2 = (f32[384,768]{1,0:T(8,128)}, f32[384,1536]{1,0:T(8,128)}, bf16[2,3,64,1536]{3,2,1,0:T(8,128)(2,1)}) custom-call(s32[14]{0:T(128)} %concatenate.106.scalars, f32[384,1536]{1,0:T(8,128)} %within.2.y_in_ref, f32[384,1536]{1,0:T(8,128)} %fusion.64.gate_ref, bf16[384,1792]{1,0:T(8,128)(2,1)} %get-tuple-element.103.act_ref, ...), custom_call_target="tpu_custom_call" | custom-call | flops 905969664 | bytes 18892800 | tf_op jit(solution)/shard_map/leave/pallas_call | solution.py:709
  311.9 16.0 %enter.3 = (bf16[384,768]{1,0:T(8,128)(2,1)}, bf16[400,1792]{1,0:T(8,128)(2,1)}, bf16[384,1792]{1,0:T(8,128)(2,1)}, bf16[384,1792]{1,0:T(8,128)(2,1)}, f32[384,1...) custom-call(s32[14]{0:T(128)} %concatenate.106.scalars, ...), custom_call_target="tpu_custom_call" | custom-call | flops 1132462080 | bytes 13995008 | tf_op jit(solution)/shard_map/enter/pallas_call | solution.py:709
  367.7 7.0 within.3.y_in_ref
  380.5 11.2 %leave.3 = (f32[384,768]{1,0:T(8,128)}, f32[384,1536]{1,0:T(8,128)}, bf16[2,3,64,1536]{3,2,1,0:T(8,128)(2,1)}) custom-call(s32[14]{0:T(128)} %concatenate.106.scalars, f32[384,1536]{1,0:T(8,128)} %within.3.y_in_ref, f32[384,1536]{1,0:T(8,128)} %fusion.65.gate_ref, bf16[384,1792]{1,0:T(8,128)(2,1)} %get-tuple-element.118.act_ref, ...), custom_call_target="tpu_custom_call" | custom-call | flops 905969664 | bytes 18892800 | tf_op jit(solution)/shard_map/leave/pallas_call | solution.py:709
  391.6 13.1 %gate_back.2 = (bf16[384,768]{1,0:T(8,128)(2,1)}, bf16[384,1536]{1,0:T(8,128)(2,1)}, bf16[384,1536]{1,0:T(8,128)(2,1)}, bf16[384,1536]{1,0:T(8,128)(2,1)}, f32[8...) custom-call(s32[14]{0:T(128)} %concatenate.106.scalars, ...), custom_call_target="tpu_custom_call" | custom-call | flops 905969664 | bytes 18401280 | tf_op jit(solution)/shard_map/gate_back/pallas_call | solution.py:709
  438.4 15.9 %within_back.2 = (f32[384,1536]{1,0:T(8,128)}, f32[384,256]{1,0:T(8,128)}, f32[384,128]{1,0:T(8,128)}, f32[384,128]{1,0:T(8,128)}) custom-call(s32[14]{0:T(128)} %concatenate.106.scalars, bf16[384,1792]{1,0:T(8,128)(2,1)} %get-tuple-element.118.act_ref, f32[384,128]{1,0:T(8,128)} %get-tuple-element.119.dt_ref, f32[384,128]{1,0:T(8,128)} %get-tuple-element.120.kum_ref, ...), custom_call_target="tpu_custom_call" | custom-call | flops 301989888 | bytes 6100992 | tf_op jit(solution)/shard_map/within_back/pallas_call | solution.py:709
  460.5 13.7 %across_back.2 = (bf16[384,1792]{1,0:T(8,128)(2,1)}, bf16[384,128]{1,0:T(8,128)(2,1)}, f32[8,128]{1,0:T(8,128)}) custom-call(s32[14]{0:T(128)} %concatenate.106.scalars, bf16[384,1792]{1,0:T(8,128)(2,1)} %get-tuple-element.118.act_ref, f32[384,128]{1,0:T(8,128)} %get-tuple-element.119.dt_ref, f32[384,128]{1,0:T(8,128)} %get-tuple-element.120.kum_ref, ...), custom_call_target="tpu_custom_call" | custom-call | flops 301989888 | bytes 14667776 | tf_op jit(solution)/shard_map/across_back/pallas_call | solution.py:709
  487.6 11.2 %proj_back.2 = (bf16[384,1920]{1,0:T(8,128)(2,1)}, bf16[768,1920]{1,0:T(8,128)(2,1)}) custom-call(s32[14]{0:T(128)} %concatenate.106.scalars, bf16[384,1792]{1,0:T(8,128)(2,1)} %get-tuple-element.152.dpre_ref, bf16[8,1792]{1,0:T(8,128)(2,1)} %copy-done.98, bf16[8,1792]{1,0:T(8,128)(2,1)} %copy-done.99, f32[8,1792]{1,0:T(8,128)} %get-tuple-element.340.taps_ref, ...), custom_call_target="tpu_custom_call" | custom-call | flops 1132462080 | bytes 6602752 | tf_op jit(solution)/shard_map/proj_back/pallas_call | solution.py:709
  498.8 7.7 norm_back.2
  506.5 13.1 %gate_back.3 = (bf16[384,768]{1,0:T(8,128)(2,1)}, bf16[384,1536]{1,0:T(8,128)(2,1)}, bf16[384,1536]{1,0:T(8,128)(2,1)}, bf16[384,1536]{1,0:T(8,128)(2,1)}, f32[8...) custom-call(s32[14]{0:T(128)} %concatenate.106.scalars, ...), custom_call_target="tpu_custom_call" | custom-call | flops 905969664 | bytes 18401280 | tf_op jit(solution)/shard_map/gate_back/pallas_call | solution.py:709
  521.3 7.5 taps_back.3
  580.8 15.8 %within_back.3 = (f32[384,1536]{1,0:T(8,128)}, f32[384,256]{1,0:T(8,128)}, f32[384,128]{1,0:T(8,128)}, f32[384,128]{1,0:T(8,128)}) custom-call(s32[14]{0:T(128)} %concatenate.106.scalars, bf16[384,1792]{1,0:T(8,128)(2,1)} %get-tuple-element.103.act_ref, f32[384,128]{1,0:T(8,128)} %get-tuple-element.104.dt_ref, f32[384,128]{1,0:T(8,128)} %get-tuple-element.105.kum_ref, ...), custom_call_target="tpu_custom_call" | custom-call | flops 301989888 | bytes 6100992 | tf_op jit(solution)/shard_map/within_back/pallas_call | solution.py:709
  597.3 13.8 %across_back.3 = (bf16[384,1792]{1,0:T(8,128)(2,1)}, bf16[384,128]{1,0:T(8,128)(2,1)}, f32[8,128]{1,0:T(8,128)}) custom-call(s32[14]{0:T(128)} %concatenate.106.scalars, bf16[384,1792]{1,0:T(8,128)(2,1)} %get-tuple-element.103.act_ref, f32[384,128]{1,0:T(8,128)} %get-tuple-element.104.dt_ref, f32[384,128]{1,0:T(8,128)} %get-tuple-element.105.kum_ref, ...), custom_call_target="tpu_custom_call" | custom-call | flops 301989888 | bytes 14667776 | tf_op jit(solution)/shard_map/across_back/pallas_call | solution.py:709
  633.1 7.3 taps_back.2
  648.1 11.2 %proj_back.3 = (bf16[384,1920]{1,0:T(8,128)(2,1)}, bf16[768,1920]{1,0:T(8,128)(2,1)}) custom-call(s32[14]{0:T(128)} %concatenate.106.scalars, bf16[384,1792]{1,0:T(8,128)(2,1)} %get-tuple-element.174.dpre_ref, bf16[8,1792]{1,0:T(8,128)(2,1)} %copy-done.100, bf16[8,1792]{1,0:T(8,128)(2,1)} %copy-done.101, f32[8,1792]{1,0:T(8,128)} %get-tuple-element.341.taps_ref, ...), custom_call_target="tpu_custom_call" | custom-call | flops 1132462080 | bytes 6602752 | tf_op jit(solution)/shard_map/proj_back/pallas_call | solution.py:709
  659.4 7.8 norm_back.3
  719.9 5.4 collective-permute-done.131
  726.9 4.8 collective-permute-done.118
  732.6 5.4 collective-permute-done.117
  739.6 4.8 collective-permute-done.153
  745.3 5.4 collective-permute-done.152
  752.3 4.8 collective-permute-done.146
  758.5 4.5 collective-permute-done.145
  798.0 5.8 collective-permute-done.139
  804.9 10.4 %collective-permute-done.138 = bf16[4,24,1920]{2,1,0:T(8,128)(2,1)S(1)} collective-permute-done((bf16[4,24,1920]{2,1,0:T(8,128)(2,1)S(1)}, bf16[4,24,1920]{2,1,0:T(8,128)(2,1)S(1)}, u32[]{:S(2)}, u32[]{:S(2)}) %collective-permute-start.138) | collective-permute-done | bytes 368672 | tf_op jit(solution)/shard_map/ppermute | solution.py:723
  (798 shorter events, 538.4 us)
Async XLA Ops:
  3.8 27.7 %collective-permute-start.2 = (bf16[16,128]{1,0:T(8,128)(2,1)S(1)}, bf16[16,128]{1,0:T(8,128)(2,1)S(1)}, u32[]{:S(2)}, u32[]{:S(2)}) collective-permute-start(bf16[16,128]{1,0:T(8,128)(2,1)S(1)} %get-tuple-element.429), channel_id=1, source_target_pairs={{0,8},{1,9},{2,10},{3,11},{4,12},{5,13},{6,14},{7,15},{8,0},{9,1},... | collective-permute-start | bytes 12296 | tf_op jit(solution)/shard_map/ppermute | solution.py:723
  6.9 24.6 %collective-permute-start.3 = (bf16[16,128]{1,0:T(8,128)(2,1)S(1)}, bf16[16,128]{1,0:T(8,128)(2,1)S(1)}, u32[]{:S(2)}, u32[]{:S(2)}) collective-permute-start(bf16[16,128]{1,0:T(8,128)(2,1)S(1)} %get-tuple-element.429), channel_id=1, source_target_pairs={{0,16},{1,17},{2,18},{3,19},{4,20},{5,21},{6,22},{7,23},{8,24},{9,... | collective-permute-start | bytes 12296 | tf_op jit(solution)/shard_map/ppermute | solution.py:723
  9.4 22.0 %collective-permute-start.4 = (bf16[16,128]{1,0:T(8,128)(2,1)S(1)}, bf16[16,128]{1,0:T(8,128)(2,1)S(1)}, u32[]{:S(2)}, u32[]{:S(2)}) collective-permute-start(bf16[16,128]{1,0:T(8,128)(2,1)S(1)} %get-tuple-element.429), channel_id=1, source_target_pairs={{0,24},{1,25},{2,26},{3,27},{4,28},{5,29},{6,30},{7,31},{8,16},{9,... | collective-permute-start | bytes 12296 | tf_op jit(solution)/shard_map/ppermute | solution.py:723
  11.1 78.8 %collective-permute-start.43 = (bf16[24,1920]{1,0:T(8,128)(2,1)}, bf16[24,1920]{1,0:T(8,128)(2,1)S(1)}, u32[]{:S(2)}, u32[]{:S(2)}) collective-permute-start(bf16[24,1920]{1,0:T(8,128)(2,1)} %get-tuple-element.363), channel_id=1, source_target_pairs={{0,8},{1,9},{2,10},{3,11},{4,12},{5,13},{6,14},{7,15},{8,0},{9,1},... | collective-permute-start | bytes 276488 | tf_op jit(solution)/shard_map/ppermute | solution.py:723
  11.9 80.1 %collective-permute-start.44 = (bf16[24,1920]{1,0:T(8,128)(2,1)}, bf16[24,1920]{1,0:T(8,128)(2,1)}, u32[]{:S(2)}, u32[]{:S(2)}) collective-permute-start(bf16[24,1920]{1,0:T(8,128)(2,1)} %get-tuple-element.363), channel_id=1, source_target_pairs={{0,16},{1,17},{2,18},{3,19},{4,20},{5,21},{6,22},{7,23},{8,24},{9,... | collective-permute-start | bytes 276488 | tf_op jit(solution)/shard_map/ppermute | solution.py:723
  38.0 57.1 %collective-permute-start.45 = (bf16[24,1920]{1,0:T(8,128)(2,1)}, bf16[24,1920]{1,0:T(8,128)(2,1)}, u32[]{:S(2)}, u32[]{:S(2)}) collective-permute-start(bf16[24,1920]{1,0:T(8,128)(2,1)} %get-tuple-element.363), channel_id=1, source_target_pairs={{0,24},{1,25},{2,26},{3,27},{4,28},{5,29},{6,30},{7,31},{8,16},{9,... | collective-permute-start | bytes 276488 | tf_op jit(solution)/shard_map/ppermute | solution.py:723
  74.5 23.8 %collective-permute-start.9 = (bf16[24,1920]{1,0:T(8,128)(2,1)}, bf16[24,1920]{1,0:T(8,128)(2,1)}, u32[]{:S(2)}, u32[]{:S(2)}) collective-permute-start(bf16[24,1920]{1,0:T(8,128)(2,1)} %get-tuple-element.373), channel_id=1, source_target_pairs={{0,8},{1,9},{2,10},{3,11},{4,12},{5,13},{6,14},{7,15},{8,0},{9,1},... | collective-permute-start | bytes 276488 | tf_op jit(solution)/shard_map/ppermute | solution.py:723
  79.4 20.9 %collective-permute-start.10 = (bf16[24,1920]{1,0:T(8,128)(2,1)}, bf16[24,1920]{1,0:T(8,128)(2,1)}, u32[]{:S(2)}, u32[]{:S(2)}) collective-permute-start(bf16[24,1920]{1,0:T(8,128)(2,1)} %get-tuple-element.373), channel_id=1, source_target_pairs={{0,16},{1,17},{2,18},{3,19},{4,20},{5,21},{6,22},{7,23},{8,24},{9,... | collective-permute-start | bytes 276488 | tf_op jit(solution)/shard_map/ppermute | solution.py:723
  103.3 20.9 %collective-permute-start.20 = (bf16[4,24,1536]{2,1,0:T(8,128)(2,1)}, bf16[4,24,1536]{2,1,0:T(8,128)(2,1)S(1)}, u32[]{:S(2)}, u32[]{:S(2)}) collective-permute-start(bf16[4,24,1536]{2,1,0:T(8,128)(2,1)} %pad_maximum_fusion.3), channel_id=1, source_target_pairs={{0,4},{1,5},{2,6},{3,7},{4,0},{5,1},{6,2},{7,3},{8,12},{9,13},{10,... | collective-permute-start | bytes 884744 | tf_op jit(solution)/shard_map/ppermute | solution.py:723
  111.6 49.9 %collective-permute-start.71 = (bf16[4,48,768]{2,1,0:T(8,128)(2,1)S(1)}, bf16[4,48,768]{2,1,0:T(8,128)(2,1)S(1)}, u32[]{:S(2)}, u32[]{:S(2)}) collective-permute-start(bf16[4,48,768]{2,1,0:T(8,128)(2,1)S(1)} %copy-done.24), channel_id=1, source_target_pairs={{0,2},{1,3},{2,0},{3,1},{4,6},{5,7},{6,4},{7,5},{8,10},{9,11},{10,... | collective-permute-start | bytes 884744 | tf_op jit(solution)/shard_map/ppermute | solution.py:723
  112.4 53.8 %collective-permute-start.72 = (bf16[4,48,768]{2,1,0:T(8,128)(2,1)S(1)}, bf16[4,48,768]{2,1,0:T(8,128)(2,1)S(1)}, u32[]{:S(2)}, u32[]{:S(2)}) collective-permute-start(bf16[4,48,768]{2,1,0:T(8,128)(2,1)S(1)} %copy-done.24), channel_id=1, source_target_pairs={{0,4},{1,5},{2,6},{3,7},{4,0},{5,1},{6,2},{7,3},{8,12},{9,13},{10,... | collective-permute-start | bytes 884744 | tf_op jit(solution)/shard_map/ppermute | solution.py:723
  115.2 53.6 %collective-permute-start.73 = (bf16[4,48,768]{2,1,0:T(8,128)(2,1)S(1)}, bf16[4,48,768]{2,1,0:T(8,128)(2,1)S(1)}, u32[]{:S(2)}, u32[]{:S(2)}) collective-permute-start(bf16[4,48,768]{2,1,0:T(8,128)(2,1)S(1)} %copy-done.24), channel_id=1, source_target_pairs={{0,6},{1,7},{2,4},{3,5},{4,2},{5,3},{6,0},{7,1},{8,14},{9,15},{10,... | collective-permute-start | bytes 884744 | tf_op jit(solution)/shard_map/ppermute | solution.py:723
  165.4 23.8 %collective-permute-start.56 = (bf16[16,24,1536]{2,1,0:T(8,128)(2,1)S(1)}, bf16[16,24,1536]{2,1,0:T(8,128)(2,1)S(1)}, u32[]{:S(2)}, u32[]{:S(2)}) collective-permute-start(bf16[16,24,1536]{2,1,0:T(8,128)(2,1)S(1)} %get-tuple-element.294), channel_id=1, source_target_pairs={{0,1},{1,0},{2,3},{3,2},{4,5},{5,4},{6,7},{7,6},{8,9},{9,8},{10,11... | collective-permute-start | bytes 3538952 | tf_op jit(solution)/shard_map/ppermute | solution.py:723
  168.8 26.9 %collective-permute-start.22 = (bf16[16,24,1536]{2,1,0:T(8,128)(2,1)}, bf16[16,24,1536]{2,1,0:T(8,128)(2,1)}, u32[]{:S(2)}, u32[]{:S(2)}) collective-permute-start(bf16[16,24,1536]{2,1,0:T(8,128)(2,1)} %get-tuple-element.310), channel_id=1, source_target_pairs={{0,1},{1,0},{2,3},{3,2},{4,5},{5,4},{6,7},{7,6},{8,9},{9,8},{10,11... | collective-permute-start | bytes 3538952 | tf_op jit(solution)/shard_map/ppermute | solution.py:723
  171.8 30.2 %collective-permute-start.49 = (bf16[16,24,1920]{2,1,0:T(8,128)(2,1)}, bf16[16,24,1920]{2,1,0:T(8,128)(2,1)}, u32[]{:S(2)}, u32[]{:S(2)}) collective-permute-start(bf16[16,24,1920]{2,1,0:T(8,128)(2,1)} %get-tuple-element.242), channel_id=1, source_target_pairs={{0,1},{1,0},{2,3},{3,2},{4,5},{5,4},{6,7},{7,6},{8,9},{9,8},{10,11... | collective-permute-start | bytes 4423688 | tf_op jit(solution)/shard_map/ppermute | solution.py:723
  174.4 33.0 %collective-permute-start.15 = (bf16[16,24,1920]{2,1,0:T(8,128)(2,1)}, bf16[16,24,1920]{2,1,0:T(8,128)(2,1)}, u32[]{:S(2)}, u32[]{:S(2)}) collective-permute-start(bf16[16,24,1920]{2,1,0:T(8,128)(2,1)} %get-tuple-element.248), channel_id=1, source_target_pairs={{0,1},{1,0},{2,3},{3,2},{4,5},{5,4},{6,7},{7,6},{8,9},{9,8},{10,11... | collective-permute-start | bytes 4423688 | tf_op jit(solution)/shard_map/ppermute | solution.py:723
  187.1 32.5 %collective-permute-start = (f32[8,768]{1,0:T(8,128)S(1)}, f32[8,768]{1,0:T(8,128)S(1)}, u32[]{:S(2)}, u32[]{:S(2)}) collective-permute-start(f32[8,768]{1,0:T(8,128)S(1)} %copy-done.74), channel_id=1, source_target_pairs={{0,1},{1,2},{2,3},{3,4},{4,5},{5,6},{6,7},{7,8},{8,9},{9,10},{10,1... | collective-permute-start | bytes 73736 | tf_op jit(solution)/shard_map/ppermute | solution.py:831
  189.2 30.5 %collective-permute-start.1 = (f32[8,768]{1,0:T(8,128)S(1)}, f32[8,768]{1,0:T(8,128)S(1)}, u32[]{:S(2)}, u32[]{:S(2)}) collective-permute-start(f32[8,768]{1,0:T(8,128)S(1)} %copy-done.73), channel_id=1, source_target_pairs={{1,0},{2,1},{3,2},{4,3},{5,4},{6,5},{7,6},{8,7},{9,8},{10,9},{11,1... | collective-permute-start | bytes 73736 | tf_op jit(solution)/shard_map/ppermute | solution.py:832
  195.7 51.9 %collective-permute-start.74 = (bf16[16,48,768]{2,1,0:T(8,128)(2,1)}, bf16[16,48,768]{2,1,0:T(8,128)(2,1)}, u32[]{:S(2)}, u32[]{:S(2)}) collective-permute-start(bf16[16,48,768]{2,1,0:T(8,128)(2,1)} %copy-done.82), channel_id=1, source_target_pairs={{0,1},{1,0},{2,3},{3,2},{4,5},{5,4},{6,7},{7,6},{8,9},{9,8},{10,11... | collective-permute-start | bytes 3538952 | tf_op jit(solution)/shard_map/ppermute | solution.py:723
  202.0 57.9 %collective-permute-start.40 = (bf16[16,48,768]{2,1,0:T(8,128)(2,1)}, bf16[16,48,768]{2,1,0:T(8,128)(2,1)}, u32[]{:S(2)}, u32[]{:S(2)}) collective-permute-start(bf16[16,48,768]{2,1,0:T(8,128)(2,1)} %copy-done.80), channel_id=1, source_target_pairs={{0,1},{1,0},{2,3},{3,2},{4,5},{5,4},{6,7},{7,6},{8,9},{9,8},{10,11... | collective-permute-start | bytes 3538952 | tf_op jit(solution)/shard_map/ppermute | solution.py:723
  433.5 20.8 %collective-permute-start.82 = (bf16[16,1536]{1,0:T(8,128)(2,1)S(1)}, bf16[16,1536]{1,0:T(8,128)(2,1)S(1)}, u32[]{:S(2)}, u32[]{:S(2)}) collective-permute-start(bf16[16,1536]{1,0:T(8,128)(2,1)S(1)} %get-tuple-element.322), channel_id=1, source_target_pairs={{0,2},{1,3},{2,0},{3,1},{4,6},{5,7},{6,4},{7,5},{8,10},{9,11},{10,... | collective-permute-start | bytes 147464 | tf_op jit(solution)/shard_map/ppermute | solution.py:723
  434.9 19.5 %collective-permute-start.83 = (bf16[16,1536]{1,0:T(8,128)(2,1)S(1)}, bf16[16,1536]{1,0:T(8,128)(2,1)S(1)}, u32[]{:S(2)}, u32[]{:S(2)}) collective-permute-start(bf16[16,1536]{1,0:T(8,128)(2,1)S(1)} %get-tuple-element.321), channel_id=1, source_target_pairs={{0,4},{1,5},{2,6},{3,7},{4,0},{5,1},{6,2},{7,3},{8,12},{9,13},{10,... | collective-permute-start | bytes 147464 | tf_op jit(solution)/shard_map/ppermute | solution.py:723
  570.6 26.0 %collective-permute-start.98 = (bf16[64,1536]{1,0:T(8,128)(2,1)}, bf16[64,1536]{1,0:T(8,128)(2,1)S(1)}, u32[]{:S(2)}, u32[]{:S(2)}) collective-permute-start(bf16[64,1536]{1,0:T(8,128)(2,1)} %get-tuple-element.172), channel_id=1, source_target_pairs={{0,1},{1,0},{2,3},{3,2},{4,5},{5,4},{6,7},{7,6},{8,9},{9,8},{10,11... | collective-permute-start | bytes 589832 | tf_op jit(solution)/shard_map/ppermute | solution.py:723
  579.0 127.1 %collective-permute-start.129 = (bf16[16,24,1536]{2,1,0:T(8,128)(2,1)}, bf16[16,24,1536]{2,1,0:T(8,128)(2,1)}, u32[]{:S(2)}, u32[]{:S(2)}) collective-permute-start(bf16[16,24,1536]{2,1,0:T(8,128)(2,1)} %slice.709), channel_id=1, source_target_pairs={{0,1},{1,0},{2,3},{3,2},{4,5},{5,4},{6,7},{7,6},{8,9},{9,8},{10,11... | collective-permute-start | bytes 3538952 | tf_op jit(solution)/shard_map/ppermute | solution.py:723
  580.6 130.5 %collective-permute-start.115 = (bf16[16,24,1536]{2,1,0:T(8,128)(2,1)}, bf16[16,24,1536]{2,1,0:T(8,128)(2,1)}, u32[]{:S(2)}, u32[]{:S(2)}) collective-permute-start(bf16[16,24,1536]{2,1,0:T(8,128)(2,1)} %slice.685), channel_id=1, source_target_pairs={{0,1},{1,0},{2,3},{3,2},{4,5},{5,4},{6,7},{7,6},{8,9},{9,8},{10,11... | collective-permute-start | bytes 3538952 | tf_op jit(solution)/shard_map/ppermute | solution.py:723
  702.8 86.6 %collective-permute-start.136 = (bf16[16,24,1920]{2,1,0:T(8,128)(2,1)}, bf16[16,24,1920]{2,1,0:T(8,128)(2,1)}, u32[]{:S(2)}, u32[]{:S(2)}) collective-permute-start(bf16[16,24,1920]{2,1,0:T(8,128)(2,1)} %slice.719), channel_id=1, source_target_pairs={{0,1},{1,0},{2,3},{3,2},{4,5},{5,4},{6,7},{7,6},{8,9},{9,8},{10,11... | collective-permute-start | bytes 4423688 | tf_op jit(solution)/shard_map/ppermute | solution.py:723
  706.1 88.7 %collective-permute-start.122 = (bf16[16,24,1920]{2,1,0:T(8,128)(2,1)}, bf16[16,24,1920]{2,1,0:T(8,128)(2,1)S(1)}, u32[]{:S(2)}, u32[]{:S(2)}) collective-permute-start(bf16[16,24,1920]{2,1,0:T(8,128)(2,1)} %slice.695), channel_id=1, source_target_pairs={{0,1},{1,0},{2,3},{3,2},{4,5},{5,4},{6,7},{7,6},{8,9},{9,8},{10,11... | collective-permute-start | bytes 4423688 | tf_op jit(solution)/shard_map/ppermute | solution.py:723
  792.9 22.4 %collective-permute-start.138 = (bf16[4,24,1920]{2,1,0:T(8,128)(2,1)S(1)}, bf16[4,24,1920]{2,1,0:T(8,128)(2,1)S(1)}, u32[]{:S(2)}, u32[]{:S(2)}) collective-permute-start(bf16[4,24,1920]{2,1,0:T(8,128)(2,1)S(1)} %get-tuple-element.213), channel_id=1, source_target_pairs={{0,4},{1,5},{2,6},{3,7},{4,0},{5,1},{6,2},{7,3},{8,12},{9,13},{10,... | collective-permute-start | bytes 1105928 | tf_op jit(solution)/shard_map/ppermute | solution.py:723
  793.9 21.3 %collective-permute-start.137 = (bf16[4,24,1920]{2,1,0:T(8,128)(2,1)S(1)}, bf16[4,24,1920]{2,1,0:T(8,128)(2,1)S(1)}, u32[]{:S(2)}, u32[]{:S(2)}) collective-permute-start(bf16[4,24,1920]{2,1,0:T(8,128)(2,1)S(1)} %get-tuple-element.211), channel_id=1, source_target_pairs={{0,2},{1,3},{2,0},{3,1},{4,6},{5,7},{6,4},{7,5},{8,10},{9,11},{10,... | collective-permute-start | bytes 1105928 | tf_op jit(solution)/shard_map/ppermute | solution.py:723
  795.3 24.3 %collective-permute-start.125 = (bf16[4,24,1920]{2,1,0:T(8,128)(2,1)S(1)}, bf16[4,24,1920]{2,1,0:T(8,128)(2,1)S(1)}, u32[]{:S(2)}, u32[]{:S(2)}) collective-permute-start(bf16[4,24,1920]{2,1,0:T(8,128)(2,1)S(1)} %get-tuple-element.209), channel_id=1, source_target_pairs={{0,6},{1,7},{2,4},{3,5},{4,2},{5,3},{6,0},{7,1},{8,14},{9,15},{10,... | collective-permute-start | bytes 1105928 | tf_op jit(solution)/shard_map/ppermute | solution.py:723
  796.9 27.5 %collective-permute-start.124 = (bf16[4,24,1920]{2,1,0:T(8,128)(2,1)S(1)}, bf16[4,24,1920]{2,1,0:T(8,128)(2,1)S(1)}, u32[]{:S(2)}, u32[]{:S(2)}) collective-permute-start(bf16[4,24,1920]{2,1,0:T(8,128)(2,1)S(1)} %get-tuple-element.210), channel_id=1, source_target_pairs={{0,4},{1,5},{2,6},{3,7},{4,0},{5,1},{6,2},{7,3},{8,12},{9,13},{10,... | collective-permute-start | bytes 1105928 | tf_op jit(solution)/shard_map/ppermute | solution.py:723
  803.7 20.7 %collective-permute-start.123 = (bf16[4,24,1920]{2,1,0:T(8,128)(2,1)S(1)}, bf16[4,24,1920]{2,1,0:T(8,128)(2,1)S(1)}, u32[]{:S(2)}, u32[]{:S(2)}) collective-permute-start(bf16[4,24,1920]{2,1,0:T(8,128)(2,1)S(1)} %get-tuple-element.208), channel_id=1, source_target_pairs={{0,2},{1,3},{2,0},{3,1},{4,6},{5,7},{6,4},{7,5},{8,10},{9,11},{10,... | collective-permute-start | bytes 1105928 | tf_op jit(solution)/shard_map/ppermute | solution.py:723
  (234 other events, 2002.2 us)
